TPU v7x, 128 devices: a whole 4x4x4 slice. The times are simulated.
128 devices in a mesh: group: 4 (over y), member: 32 (over z, x, core).
Axes of the slice: x: 4, y: 4, z: 4, core: 2. Of those that a mesh axis runs over, the one named last changes fastest.
Arguments:
- memory: float32 [131072, 512], P(('group', 'member')), may hold values from -3 to 3
- source_owner: int32 [32768, 1], P(('group', 'member')), may hold values from 0 to 127; in each aligned block of 256 rows (0 to 255, 256 to 511, ...) at most 4 rows name the same one
- target_owner: int32 [32768, 1], P(('group', 'member')), may hold values from 0 to 127; in each aligned block of 256 rows (0 to 255, 256 to 511, ...) at most 4 rows name the same one
- source_row: int32 [32768], P(('group', 'member')), may hold values from 0 to 1023
- target_row: int32 [32768], P(('group', 'member')), may hold values from 0 to 1023
- event_time: int32 [32768], P(('group', 'member')), may hold values from 0 to 2047
- query_rows: int32 [16384], P(('group', 'member')), may hold values from 0 to 1023
- link_member: int32 [163840, 1], P(('group', 'member')), may hold values from 0 to 31; in each aligned block of 1280 rows (0 to 1279, 1280 to 2559, ...) at most 80 rows name the same one
- link_slot: int32 [163840], P(('group', 'member')), may hold values from 0 to 127
- link_delta: int32 [163840], P(('group', 'member')), may hold values from 0 to 2047
- frequency: float32 [128], replicated, may hold values from 0.001 to 0.5
- time_phase: float32 [128], replicated, may hold values from -3.140625 to 3.140625
- msg_weight: bfloat16 [1152, 512], replicated, may hold values from -0.1875 to 0.1875
- msg_bias: float32 [512], replicated, may hold values from -3 to 3
- input_weight: bfloat16 [512, 1536], replicated, may hold values from -0.25 to 0.25
- state_weight: bfloat16 [512, 1536], replicated, may hold values from -0.25 to 0.25
- input_bias: float32 [1536], replicated, may hold values from -3 to 3
- state_bias: float32 [1536], replicated, may hold values from -3 to 3
- query_weight: bfloat16 [2, 640, 512], replicated, may hold values from -0.25 to 0.25
- key_weight: bfloat16 [2, 640, 512], replicated, may hold values from -0.25 to 0.25
- value_weight: bfloat16 [2, 640, 512], replicated, may hold values from -0.25 to 0.25
- merge_weight: bfloat16 [2, 1024, 512], replicated, may hold values from -0.1875 to 0.1875
- merge_bias: float32 [2, 512], replicated, may hold values from -3 to 3
Outputs:
- new_memory: float32 [131072, 512], P(('group', 'member'))
- embedding: bfloat16 [16384, 512], P(('group', 'member'))
Inputs may be any that keep to these rules, and one draw needn't show every extreme that they name: `source_owner`: among the events of one device at most 4 have their source owned by one device, and some device's events reach it. `target_owner`: among the events of one device at most 4 have their destination owned by one device, and some device's events reach it. `link_member`: among the links of one device at most 80 point to one member, and some device's links reach it.
All inputs are finite; a program needn't handle non-finite values.
Results may differ from a plain program's by a relative error of at most 0.0065.
Values may be sent and summed in bfloat16 or wider, within the bound.
A program may use at most 128 MiB of HBM per device.

v0:
```python
import math

import jax
import jax.numpy as jnp
from jax import lax
from jax.sharding import PartitionSpec as P

HEADS = 2


def slot_numbers(owners, peer_count):
    owner_marks = (owners[:, None] == jnp.arange(peer_count, dtype=jnp.int32)[None, :]).astype(
        jnp.int32
    )
    earlier = jnp.cumsum(owner_marks, axis=0) - owner_marks
    return jnp.sum(earlier * owner_marks, axis=1)


def time_code(stamps, frequency, time_phase):
    return jnp.cos(
        stamps.astype(jnp.float32)[:, None] * frequency[None, :] + time_phase[None, :]
    ).astype(jnp.bfloat16)


def gru_cell(inputs, hidden, input_weight, state_weight, input_bias, state_bias):
    row_width = hidden.shape[1]
    from_input = jnp.dot(inputs, input_weight, preferred_element_type=jnp.float32) + input_bias
    from_state = (
        jnp.dot(hidden.astype(jnp.bfloat16), state_weight, preferred_element_type=jnp.float32)
        + state_bias
    )
    reset_gate = jax.nn.sigmoid(from_input[:, :row_width] + from_state[:, :row_width])
    update_gate = jax.nn.sigmoid(
        from_input[:, row_width : 2 * row_width] + from_state[:, row_width : 2 * row_width]
    )
    candidate = jnp.tanh(
        from_input[:, 2 * row_width :] + reset_gate * from_state[:, 2 * row_width :]
    )
    return (1.0 - update_gate) * candidate + update_gate * hidden


def attend(
    feats,
    neighbours,
    delta_code,
    self_code,
    query_weight,
    key_weight,
    value_weight,
    merge_weight,
    merge_bias,
    head_count,
):
    query_count, row_width = feats.shape
    fanout = neighbours.shape[1]
    head_size = row_width // head_count
    query_vec = jnp.dot(
        jnp.concatenate([feats, self_code], 1), query_weight, preferred_element_type=jnp.float32
    )
    key_input = jnp.concatenate([neighbours, delta_code], 2).reshape(query_count * fanout, -1)
    key_vec = jnp.dot(key_input, key_weight, preferred_element_type=jnp.float32).reshape(
        query_count, fanout, head_count, head_size
    )
    value_vec = jnp.dot(key_input, value_weight, preferred_element_type=jnp.float32).reshape(
        query_count, fanout, head_count, head_size
    )
    query_vec = query_vec.reshape(query_count, 1, head_count, head_size)
    scores = jnp.sum(query_vec * key_vec, axis=3) / math.sqrt(head_size)
    weights = jnp.exp(scores)
    weights = weights / jnp.sum(weights, axis=1, keepdims=True)
    mixed_out = (
        jnp.sum(weights[..., None] * value_vec, axis=1)
        .reshape(query_count, row_width)
        .astype(jnp.bfloat16)
    )
    merged = (
        jnp.dot(
            jnp.concatenate([mixed_out, feats], 1), merge_weight, preferred_element_type=jnp.float32
        )
        + merge_bias
    )
    return jax.nn.relu(merged).astype(jnp.bfloat16)


def on_device(
    memory,
    source_owner,
    target_owner,
    source_row,
    target_row,
    event_time,
    query_rows,
    link_member,
    link_slot,
    link_delta,
    frequency,
    time_phase,
    msg_weight,
    msg_bias,
    input_weight,
    state_weight,
    input_bias,
    state_bias,
    query_weight,
    key_weight,
    value_weight,
    merge_weight,
    merge_bias,
):
    peer_count = lax.axis_size(("group", "member"))
    member_count = lax.axis_size("member")
    event_count = source_row.shape[0]
    node_rows, row_width = memory.shape
    capacity = max(2, 2 * event_count // peer_count)
    source_place = source_owner[:, 0] * (2 * capacity) + slot_numbers(
        source_owner[:, 0], peer_count
    )
    target_place = (
        target_owner[:, 0] * (2 * capacity)
        + capacity
        + slot_numbers(target_owner[:, 0], peer_count)
    )
    slot_index = jnp.concatenate([source_place, target_place])
    wanted = (
        jnp.full((peer_count * 2 * capacity,), -1, jnp.int32)
        .at[slot_index]
        .set(jnp.concatenate([source_row, target_row]))
    )
    requests_in = lax.all_to_all(
        wanted.reshape(peer_count, 2 * capacity),
        ("group", "member"),
        split_axis=0,
        concat_axis=0,
        tiled=True,
    ).reshape(-1)
    live_slots = requests_in >= 0
    picked = (
        memory[jnp.maximum(requests_in, 0)]
        .astype(jnp.bfloat16)
        .reshape(peer_count, 2 * capacity, row_width)
    )
    fetched = lax.all_to_all(picked, ("group", "member"), split_axis=0, concat_axis=0, tiled=True)
    fetched = fetched.reshape(-1, row_width)
    source_mem = fetched[source_place]
    target_mem = fetched[target_place]
    stamp_code = time_code(event_time, frequency, time_phase)
    inputs = jnp.concatenate(
        [
            jnp.concatenate([source_mem, target_mem, stamp_code], 1),
            jnp.concatenate([target_mem, source_mem, stamp_code], 1),
        ],
        0,
    )
    message = jax.nn.relu(
        jnp.dot(inputs, msg_weight, preferred_element_type=jnp.float32) + msg_bias
    ).astype(jnp.bfloat16)
    outbound = (
        jnp.zeros((peer_count * 2 * capacity, row_width), jnp.bfloat16).at[slot_index].set(message)
    )
    inbound = lax.all_to_all(
        outbound.reshape(peer_count, 2 * capacity, row_width),
        ("group", "member"),
        split_axis=0,
        concat_axis=0,
        tiled=True,
    )
    inbound = inbound.reshape(-1, row_width)
    target_rows = jnp.where(live_slots, requests_in, node_rows)
    summed = jax.ops.segment_sum(
        inbound.astype(jnp.float32), target_rows, num_segments=node_rows + 1
    )[:node_rows]
    touched = jax.ops.segment_sum(
        live_slots.astype(jnp.float32), target_rows, num_segments=node_rows + 1
    )[:node_rows]
    mean_msg = (summed / jnp.maximum(touched, 1.0)[:, None]).astype(jnp.bfloat16)
    refreshed = gru_cell(mean_msg, memory, input_weight, state_weight, input_bias, state_bias)
    new_memory = jnp.where(touched[:, None] > 0, refreshed, memory)
    query_count = query_rows.shape[0]
    link_count = link_member.shape[0]
    fanout = link_count // query_count
    head_count = query_weight.shape[2] // (query_weight.shape[2] // HEADS)
    features0 = new_memory[query_rows].astype(jnp.bfloat16)
    delta_code = time_code(link_delta, frequency, time_phase).reshape(query_count, fanout, -1)
    self_code = time_code(jnp.zeros((query_count,), jnp.int32), frequency, time_phase)
    owner_member = link_member[:, 0]
    room_each = max(2, 2 * link_count // member_count)
    spot_index = owner_member * room_each + slot_numbers(owner_member, member_count)
    request_out = jnp.full((member_count * room_each,), -1, jnp.int32).at[spot_index].set(link_slot)
    served_rows = lax.all_to_all(
        request_out.reshape(member_count, room_each),
        "member",
        split_axis=0,
        concat_axis=0,
        tiled=True,
    ).reshape(-1)
    served_rows = jnp.maximum(served_rows, 0)

    def fetch_rows(feature_rows):
        returned = lax.all_to_all(
            feature_rows[served_rows].reshape(member_count, room_each, row_width),
            "member",
            split_axis=0,
            concat_axis=0,
            tiled=True,
        )
        return returned.reshape(-1, row_width)[spot_index].reshape(query_count, fanout, row_width)

    features1 = attend(
        features0,
        fetch_rows(features0),
        delta_code,
        self_code,
        query_weight[0],
        key_weight[0],
        value_weight[0],
        merge_weight[0],
        merge_bias[0],
        head_count,
    )
    embedding = attend(
        features1,
        fetch_rows(features1),
        delta_code,
        self_code,
        query_weight[1],
        key_weight[1],
        value_weight[1],
        merge_weight[1],
        merge_bias[1],
        head_count,
    )
    return (new_memory, embedding)


def solution(mesh):
    in_specs = (
        P(("group", "member"), None),
        P(("group", "member"), None),
        P(("group", "member"), None),
        P(("group", "member")),
        P(("group", "member")),
        P(("group", "member")),
        P(("group", "member")),
        P(("group", "member"), None),
        P(("group", "member")),
        P(("group", "member")),
        P(),
        P(),
        P(),
        P(),
        P(),
        P(),
        P(),
        P(),
        P(),
        P(),
        P(),
        P(),
        P(),
    )
    out_specs = (P(("group", "member"), None), P(("group", "member"), None))
    return jax.shard_map(
        on_device, mesh=mesh, in_specs=in_specs, out_specs=out_specs, check_vma=False
    )
```

profile of v0, /device:TPU:1, one launch (start us, length us, event | category | flops | bytes accessed | tf_op | source)
XLA Modules:
  0.0 250.4 jit_solution(9907995259448110760)
XLA Ops:
  6.1 2.4 scatter_custom_fusion
  9.3 11.5 %all-to-all-start = ((s32[128,1,8]{2,1,0:T(1,128)}), s32[128,1,8]{2,1,0:T(1,128)S(1)}, u32[]{:S(2)}, u32[]{:S(2)}) async-start(s32[128,1,8]{2,1,0:T(1,128)} %bitcast.13), calls=%async_computation | async-start | bytes 131072 | tf_op jit(solution)/shard_map/all_to_all | solution.py:129
  20.8 9.1 %reduce-window.26 = s32[32,10,128]{2,1,0:T(8,128)S(1)} reduce-window(s32[32,10,128]{2,1,0:T(8,128)S(1)} %fusion.56, s32[]{:T(128)} %constant.18.clone.1), window={size=1x1x128 pad=0_0x0_0x127_0}, to_apply=%region_10.11 | reduce-window | flops 5201920 | bytes 327684 | tf_op jit(solution)/shard_map/reduce-window.4
  32.1 6.7 %gather_fusion = bf16[1024,512]{1,0:T(8,128)(2,1)} fusion(f32[1024,512]{1,0:T(8,128)} %param.23, s32[1024]{0:T(1024)S(1)} %broadcast_clamp_fusion), kind=kCustom, calls=%fused_computation | custom fusion | bytes 2101248 | tf_op jit(solution)/shard_map/gather | solution.py:138
  38.8 9.8 %all-to-all-start.1 = ((bf16[128,8,512]{2,1,0:T(8,128)(2,1)}), bf16[128,8,512]{2,1,0:T(8,128)(2,1)S(1)}, u32[]{:S(2)}, u32[]{:S(2)}) async-start(bf16[128,8,512]{2,1,0:T(8,128)(2,1)} %bitcast.158), calls=%async_computation.1 | async-start | bytes 2097152 | tf_op jit(solution)/shard_map/all_to_all | solution.py:142
  48.6 5.4 %scatter_custom_fusion.4 = s32[2560]{0:T(1024)S(1)} fusion(s32[1280]{0:T(1024)S(1)} %fusion.83, s32[1280]{0:T(1024)} %param.31, s32[]{:T(128)} %constant.16.clone.1), kind=kCustom, calls=%fused_computation.134 | custom fusion | bytes 10752 | tf_op jit(solution)/shard_map/scatter | solution.py:188
  55.3 6.0 %convolution_add_fusion = f32[1024,1536]{1,0:T(8,128)} fusion(bf16[512,1536]{1,0:T(8,128)(2,1)S(1)} %copy-done, f32[1536]{0:T(1024)S(1)} %copy-done.19, f32[1024,512]{1,0:T(8,128)} %param.23), kind=kOutput, calls=%fused_computation.13 | convolution fusion | flops 1612709888 | bytes 9967616 | tf_op jit(solution)/shard_map/dot_general | solution.py:29
  61.3 6.6 %all-to-all-done.1 = bf16[128,8,512]{2,1,0:T(8,128)(2,1)S(1)} async-done(((bf16[128,8,512]{2,1,0:T(8,128)(2,1)}), bf16[128,8,512]{2,1,0:T(8,128)(2,1)S(1)}, u32[]{:S(2)}, u32[]{:S(2)}) %all-to-all-start.1) | async-done | bytes 1048608 | tf_op jit(solution)/shard_map/all_to_all | solution.py:142
  67.9 4.4 %all-to-all-start.3 = ((s32[32,1,80]{2,1,0:T(1,128)}), s32[32,1,80]{2,1,0:T(1,128)S(1)}, u32[]{:S(2)}, u32[]{:S(2)}) async-start(s32[32,1,80]{2,1,0:T(1,128)} %all_to_all.28), calls=%async_computation.3 | async-start | bytes 32768 | tf_op jit(solution)/shard_map/all_to_all | solution.py:189
  72.3 1.2 gather_fusion.1
  73.4 1.2 gather_fusion.2
  74.6 2.1 fusion.19
  76.7 3.5 %scatter_custom_fusion.2 = bf16[1024,512]{1,0:T(8,128)(2,1)} fusion(s32[512]{0:T(512)S(1)} %bitcast.191, bf16[512,512]{1,0:T(8,128)(2,1)S(1)} %fusion.19, bf16[]{:T(256)} %constant.22.clone.1), kind=kCustom, calls=%fused_computation.79 | custom fusion | bytes 1048578 | tf_op jit(solution)/shard_map/scatter | solution.py:158
  80.2 7.4 %all-to-all-start.2 = ((bf16[128,8,512]{2,1,0:T(8,128)(2,1)}), bf16[128,8,512]{2,1,0:T(8,128)(2,1)S(1)}, u32[]{:S(2)}, u32[]{:S(2)}) async-start(bf16[128,8,512]{2,1,0:T(8,128)(2,1)} %bitcast.20), calls=%async_computation.2 | async-start | bytes 2097152 | tf_op jit(solution)/shard_map/all_to_all | solution.py:160
  87.9 5.9 %scatter_custom_fusion.1 = f32[1025]{0:T(1024)S(1)} fusion(s32[1024]{0:T(1024)S(1)} %bitcast.186, f32[1024]{0:T(1024)S(1)} %reshape.401, f32[]{:T(128)} %constant.15.clone.1), kind=kCustom, calls=%fused_computation.146 | custom fusion | flops 1024 | bytes 4104 | tf_op jit(solution)/shard_map/scatter-add | solution.py:172
  94.0 12.9 %all-to-all-done.2 = bf16[128,8,512]{2,1,0:T(8,128)(2,1)S(1)} async-done(((bf16[128,8,512]{2,1,0:T(8,128)(2,1)}), bf16[128,8,512]{2,1,0:T(8,128)(2,1)S(1)}, u32[]{:S(2)}, u32[]{:S(2)}) %all-to-all-start.2) | async-done | bytes 1048608 | tf_op jit(solution)/shard_map/all_to_all | solution.py:160
  106.9 8.2 %scatter_custom_fusion.3 = f32[1025,512]{1,0:T(8,128)} fusion(s32[1024]{0:T(1024)S(1)} %bitcast.187, f32[]{:T(128)} %constant.15.clone.1, bf16[128,8,512]{2,1,0:T(8,128)(2,1)S(1)} %all-to-all-done.2), kind=kCustom, calls=%fused_computation.39 | custom fusion | flops 1048576 | bytes 3147780 | tf_op jit(solution)/shard_map/scatter-add | solution.py:169
  115.1 4.0 %convolution_add_fusion.1 = f32[1024,1536]{1,0:T(8,128)S(1)} fusion(bf16[512,1536]{1,0:T(8,128)(2,1)} %param.37, f32[1536]{0:T(1024)S(1)} %copy-done.20, f32[1025,512]{1,0:T(8,128)} %scatter_custom_fusion.3, f32[1024]{0:T(1024)S(1)} %slice_maximum_fusion), kind=kOutput, calls=%fused_computation.14 | convolution fusion | flops 1613234176 | bytes 9971712 | tf_op jit(solution)/shard_map/dot_general | solution.py:27
  119.1 4.8 %fusion.4 = f32[1024,512]{1,0:T(8,128)} fusion(f32[1024,512]{1,0:T(8,128)S(1)} %copy-done.1, f32[1024,1536]{1,0:T(8,128)} %convolution_add_fusion, f32[1024,1536]{1,0:T(8,128)S(1)} %convolution_add_fusion.1, pred[1024]{0:T(1024)(128)(4,1)S(1)} %slice_compare_fusion), kind=kLoop, calls=%fused_computation.26 | loop fusion | flops 7864320 | bytes 16778240 | tf_op jit(solution)/shard_map/jit(_where)/select_n | solution.py:177
  123.9 2.5 gather_fusion.3
  126.3 8.2 %gather_fusion.4 = bf16[2560,512]{1,0:T(8,128)(2,1)} fusion(bf16[128,512]{1,0:T(8,128)(2,1)S(1)} %gather_fusion.3, s32[3072]{0:T(1024)S(1)} %pad_clamp_fusion), kind=kCustom, calls=%fused_computation.4 | custom fusion | bytes 5253120 | tf_op jit(solution)/shard_map/gather | solution.py:200
  134.6 5.3 %all-to-all-start.4 = ((bf16[32,80,512]{2,1,0:T(8,128)(2,1)}), bf16[32,80,512]{2,1,0:T(8,128)(2,1)}, u32[]{:S(2)}, u32[]{:S(2)}) async-start(bf16[32,80,512]{2,1,0:T(8,128)(2,1)} %bitcast.156), calls=%async_computation.4 | async-start | bytes 5242880 | tf_op jit(solution)/shard_map/all_to_all | solution.py:199
  139.8 2.2 slice_bitcast_fusion.2
  142.6 2.2 slice_bitcast_fusion.1
  144.8 1.1 copy.58
  145.9 2.2 slice_bitcast_fusion
  148.2 1.1 copy.59
  149.3 2.3 cosine_convert_fusion
  151.7 1.1 fusion.60
  152.8 20.7 %all-to-all-done.4 = bf16[32,80,512]{2,1,0:T(8,128)(2,1)} async-done(((bf16[32,80,512]{2,1,0:T(8,128)(2,1)}), bf16[32,80,512]{2,1,0:T(8,128)(2,1)}, u32[]{:S(2)}, u32[]{:S(2)}) %all-to-all-start.4) | async-done | bytes 2621472 | tf_op jit(solution)/shard_map/all_to_all | solution.py:199
  173.5 6.2 %gather_fusion.5 = bf16[1280,512]{1,0:T(8,128)(2,1)S(1)} fusion(bf16[2560,512]{1,0:T(8,128)(2,1)} %bitcast.29, s32[2048]{0:T(1024)S(1)} %pad_clamp_fusion.1), kind=kCustom, calls=%fused_computation.5 | custom fusion | bytes 2626560 | tf_op jit(solution)/shard_map/gather | solution.py:206
  179.7 1.6 concatenate.68
  181.3 2.4 copy.57
  183.7 1.3 multiply_reduce_fusion.3
  185.1 1.2 multiply_reduce_fusion.2
  187.0 8.2 %gather_fusion.6 = bf16[2560,512]{1,0:T(8,128)(2,1)} fusion(bf16[128,512]{1,0:T(8,128)(2,1)S(1)} %fusion.33, s32[3072]{0:T(1024)S(1)} %pad_clamp_fusion), kind=kCustom, calls=%fused_computation.6 | custom fusion | bytes 5253120 | tf_op jit(solution)/shard_map/gather | solution.py:200
  195.2 7.3 %all-to-all-start.5 = ((bf16[32,80,512]{2,1,0:T(8,128)(2,1)}), bf16[32,80,512]{2,1,0:T(8,128)(2,1)}, u32[]{:S(2)}, u32[]{:S(2)}) async-start(bf16[32,80,512]{2,1,0:T(8,128)(2,1)} %bitcast.157), calls=%async_computation.5 | async-start | bytes 5242880 | tf_op jit(solution)/shard_map/all_to_all | solution.py:199
  202.6 1.1 copy.61
  203.7 1.1 copy.63
  204.7 2.2 copy.64
  206.9 1.1 fusion.62
  208.0 28.2 %all-to-all-done.5 = bf16[32,80,512]{2,1,0:T(8,128)(2,1)} async-done(((bf16[32,80,512]{2,1,0:T(8,128)(2,1)}), bf16[32,80,512]{2,1,0:T(8,128)(2,1)}, u32[]{:S(2)}, u32[]{:S(2)}) %all-to-all-start.5) | async-done | bytes 2621472 | tf_op jit(solution)/shard_map/all_to_all | solution.py:199
  236.2 6.2 %gather_fusion.7 = bf16[1280,512]{1,0:T(8,128)(2,1)S(1)} fusion(bf16[2560,512]{1,0:T(8,128)(2,1)} %bitcast.48, s32[2048]{0:T(1024)S(1)} %pad_clamp_fusion.1), kind=kCustom, calls=%fused_computation.7 | custom fusion | bytes 2626560 | tf_op jit(solution)/shard_map/gather | solution.py:206
  242.4 1.6 concatenate.72
  244.0 2.4 copy.62
  246.4 1.3 multiply_reduce_fusion.1
  247.8 1.2 multiply_reduce_fusion
  249.4 1.0 fusion.34
  (113 shorter events, 11.7 us)
Async XLA Ops:
  0.6 54.6 %copy-start = (bf16[512,1536]{1,0:T(8,128)(2,1)S(1)}, bf16[512,1536]{1,0:T(8,128)(2,1)}, u32[]{:S(2)}) copy-start(bf16[512,1536]{1,0:T(8,128)(2,1)} %param.38) | copy-start | bytes 4718596
  0.6 20.1 %copy-start.11 = (s32[1280,1]{0,1:T(1,128)S(1)}, s32[1280,1]{0,1:T(1,128)}, u32[]{:S(2)}) copy-start(s32[1280,1]{0,1:T(1,128)} %param.30) | copy-start | bytes 15364
  1.8 28.8 %copy-start.16 = (s32[256]{0:T(256)S(1)}, s32[256]{0:T(256)}, u32[]{:S(2)}) copy-start(s32[256]{0:T(256)} %param.28) | copy-start | bytes 3076
  9.3 21.3 %all-to-all-start = ((s32[128,1,8]{2,1,0:T(1,128)}), s32[128,1,8]{2,1,0:T(1,128)S(1)}, u32[]{:S(2)}, u32[]{:S(2)}) async-start(s32[128,1,8]{2,1,0:T(1,128)} %bitcast.13), calls=%async_computation | async-start | bytes 131072 | tf_op jit(solution)/shard_map/all_to_all | solution.py:129
  38.8 16.0 %copy-start.14 = (f32[128]{0:T(128)S(1)}, f32[128]{0:T(128)}, u32[]{:S(2)}) copy-start(f32[128]{0:T(128)} %param.34) | copy-start | bytes 1540
  38.8 16.0 %copy-start.15 = (f32[128]{0:T(128)S(1)}, f32[128]{0:T(128)}, u32[]{:S(2)}) copy-start(f32[128]{0:T(128)} %param.33) | copy-start | bytes 1540
  38.8 16.5 %copy-start.19 = (f32[1536]{0:T(1024)S(1)}, f32[1536]{0:T(1024)}, u32[]{:S(2)}) copy-start(f32[1536]{0:T(1024)} %param.40) | copy-start | bytes 18436
  38.8 29.1 %all-to-all-start.1 = ((bf16[128,8,512]{2,1,0:T(8,128)(2,1)}), bf16[128,8,512]{2,1,0:T(8,128)(2,1)S(1)}, u32[]{:S(2)}, u32[]{:S(2)}) async-start(bf16[128,8,512]{2,1,0:T(8,128)(2,1)} %bitcast.158), calls=%async_computation.1 | async-start | bytes 2097152 | tf_op jit(solution)/shard_map/all_to_all | solution.py:142
  67.9 12.3 %all-to-all-start.3 = ((s32[32,1,80]{2,1,0:T(1,128)}), s32[32,1,80]{2,1,0:T(1,128)S(1)}, u32[]{:S(2)}, u32[]{:S(2)}) async-start(s32[32,1,80]{2,1,0:T(1,128)} %all_to_all.28), calls=%async_computation.3 | async-start | bytes 32768 | tf_op jit(solution)/shard_map/all_to_all | solution.py:189
  72.3 2.3 copy-start.21
  76.7 10.9 %copy-start.22 = (s32[128]{0:T(128)S(1)}, s32[128]{0:T(128)}, u32[]{:S(2)}) copy-start(s32[128]{0:T(128)} %param.29) | copy-start | bytes 1540
  80.2 26.7 %all-to-all-start.2 = ((bf16[128,8,512]{2,1,0:T(8,128)(2,1)}), bf16[128,8,512]{2,1,0:T(8,128)(2,1)S(1)}, u32[]{:S(2)}, u32[]{:S(2)}) async-start(bf16[128,8,512]{2,1,0:T(8,128)(2,1)} %bitcast.20), calls=%async_computation.2 | async-start | bytes 2097152 | tf_op jit(solution)/shard_map/all_to_all | solution.py:160
  87.6 27.5 %copy-start.20 = (f32[1536]{0:T(1024)S(1)}, f32[1536]{0:T(1024)}, u32[]{:S(2)}) copy-start(f32[1536]{0:T(1024)} %param.39) | copy-start | bytes 18436
  115.1 4.1 %copy-start.1 = (f32[1024,512]{1,0:T(8,128)S(1)}, f32[1024,512]{1,0:T(8,128)}, u32[]{:S(2)}) copy-start(f32[1024,512]{1,0:T(8,128)} %param.23) | copy-start | bytes 6291460
  134.6 38.9 %all-to-all-start.4 = ((bf16[32,80,512]{2,1,0:T(8,128)(2,1)}), bf16[32,80,512]{2,1,0:T(8,128)(2,1)}, u32[]{:S(2)}, u32[]{:S(2)}) async-start(bf16[32,80,512]{2,1,0:T(8,128)(2,1)} %bitcast.156), calls=%async_computation.4 | async-start | bytes 5242880 | tf_op jit(solution)/shard_map/all_to_all | solution.py:199
  139.8 2.5 %copy-start.12 = (s32[1280]{0:T(1024)S(1)}, s32[1280]{0:T(1024)}, u32[]{:S(2)}) copy-start(s32[1280]{0:T(1024)} %param.32) | copy-start | bytes 15364
  145.9 3.4 %copy-start.13 = (f32[2,512]{1,0:T(2,128)S(1)}, f32[2,512]{1,0:T(2,128)}, u32[]{:S(2)}) copy-start(f32[2,512]{1,0:T(2,128)} %param.45) | copy-start | bytes 12292
  181.3 2.4 copy-start.6
  181.3 2.4 copy-start.10
  183.7 1.4 copy-start.5
  185.1 1.6 copy-start.17
  195.2 7.3 %copy-start.2 = (bf16[512,640]{0,1:T(8,128)(2,1)S(1)}, bf16[512,640]{0,1:T(8,128)(2,1)}, u32[]{:S(2)}) copy-start(bf16[512,640]{0,1:T(8,128)(2,1)} %get-tuple-element.6) | copy-start | bytes 1966084
  195.2 8.4 %copy-start.3 = (bf16[512,640]{0,1:T(8,128)(2,1)S(1)}, bf16[512,640]{0,1:T(8,128)(2,1)}, u32[]{:S(2)}) copy-start(bf16[512,640]{0,1:T(8,128)(2,1)} %get-tuple-element.8) | copy-start | bytes 1966084
  195.2 41.0 %all-to-all-start.5 = ((bf16[32,80,512]{2,1,0:T(8,128)(2,1)}), bf16[32,80,512]{2,1,0:T(8,128)(2,1)}, u32[]{:S(2)}, u32[]{:S(2)}) async-start(bf16[32,80,512]{2,1,0:T(8,128)(2,1)} %bitcast.157), calls=%async_computation.5 | async-start | bytes 5242880 | tf_op jit(solution)/shard_map/all_to_all | solution.py:199
  203.7 3.3 %copy-start.4 = (bf16[512,640]{1,0:T(8,128)(2,1)S(1)}, bf16[512,640]{1,0:T(8,128)(2,1)}, u32[]{:S(2)}) copy-start(bf16[512,640]{1,0:T(8,128)(2,1)} %copy.61) | copy-start | bytes 1966084
  244.0 2.4 copy-start.8
  244.0 2.4 copy-start.9
  246.4 1.4 copy-start.7
  247.8 1.6 copy-start.18
where the time goes:
time: 253 us; the launch traced here: 250 us
  local copies, waits for them, and re-layouts  78.5 us (31%)
  waiting for transfers between devices  68.4 us (27%)
  starting transfers between devices  45.6 us (18%)
  other arithmetic  35.9 us (14%)
  matrix products  20.7 us (8%)
    all_to_all x2, waiting for transfers between devices, fetch_rows(): lax.all_to_all(feature_rows[served_rows].reshape(member_count, room_each,...  49 us
    gather x2, local copies, waits for them, and re-layouts, fetch_rows(): feature_rows[served_rows].reshape(member_count, room_each, row_width)  16.4 us
    all_to_all x1, waiting for transfers between devices, on_device(): lax.all_to_all(outbound.reshape(peer_count, 2 * capacity, row_width), ('g...  12.9 us
    all_to_all x2, starting transfers between devices, fetch_rows(): lax.all_to_all(feature_rows[served_rows].reshape(member_count, room_each,...  12.6 us
    gather x2, local copies, waits for them, and re-layouts, fetch_rows(): returned.reshape(-1, row_width)[spot_index]  12.4 us
    all_to_all x1, starting transfers between devices, on_device(): lax.all_to_all(wanted.reshape(peer_count, 2 * capacity), ('group', 'membe...  11.5 us
    all_to_all x1, starting transfers between devices, on_device(): lax.all_to_all(picked, ('group', 'member'), split_axis=0, concat_axis=0,...  9.76 us
    another operation x9, other arithmetic  9.74 us
  transfers between devices with their start and end apart: 6, of which 4 were waited for; matrix products, arithmetic and copies ran while one was open for 22% of the time, Pallas kernels for 0%

commit v1 on v0

v1 whole, which is shorter than its diff:
```python
import functools
import math

import jax
import jax.numpy as jnp
from jax import lax
from jax.experimental import pallas as pl
from jax.experimental.pallas import tpu as pltpu
from jax.sharding import PartitionSpec as P

MESH = pl.DeviceIdType.MESH
F32 = jnp.float32
BF16 = jnp.bfloat16
I32 = jnp.int32
HEADS = 2
FAN = 10
LANES = 128
NEG = -1e30


def iota(shape, dim):
    return lax.broadcasted_iota(I32, shape, dim)


def dot(a, b):
    return jnp.dot(a, b, preferred_element_type=F32)


def dot_t(a, b):
    return lax.dot_general(a, b, (((1,), (1,)), ((), ())), preferred_element_type=F32)


def cosine(x):
    turns = jnp.floor(x * (0.5 / math.pi) + 0.5)
    y = 0.5 * ((x - turns * 6.28125) - turns * (2.0 * math.pi - 6.28125))
    s = y * y
    p = 1.0 / 362880 - s * (1.0 / 39916800)
    p = -1.0 / 5040 + s * p
    p = 1.0 / 120 + s * p
    p = -1.0 / 6 + s * p
    sine = y + y * s * p
    return 1.0 - 2.0 * sine * sine


def column(row):
    n = row.shape[1]
    return jnp.sum(jnp.where(iota((n, n), 0) == iota((n, n), 1), row, 0.0), axis=1, keepdims=True)


def kernel(
    group_size,
    device_count,
    memory,
    s_owner,
    t_owner,
    s_row,
    t_row,
    e_time,
    q_rows,
    l_member,
    l_slot,
    l_delta,
    freq,
    phase,
    msg_w,
    msg_b,
    in_w,
    st_w,
    in_b,
    st_b,
    q_w,
    k_w,
    v_w,
    m_w,
    m_b,
    new_memory,
    embedding,
    mem,
    mem_hi,
    mem_lo,
    msg_v,
    in_v,
    st_v,
    q_v,
    k_v,
    v_v,
    m_v,
    req_out,
    req_in,
    slot_row,
    xout,
    fetched,
    yout,
    inbound,
    pick,
    place,
    msgs,
    back,
    touched,
    state,
    table,
    inverse,
    code,
    u_buf,
    cp,
    s_acc,
    acc,
    local_sem,
    out_sem,
    send_sem,
    recv_sem,
    hop_send,
    hop_recv,
):
    group = lax.axis_index("group")
    member = lax.axis_index("member")
    me = group * group_size + member
    nodes, width = mem.shape
    events = s_row.shape[1]
    queries = q_rows.shape[1]
    slots = device_count * 8
    barrier = pltpu.get_barrier_semaphore()

    def device(t):
        d = lax.rem(me + t, device_count)
        return d, {"group": lax.div(d, group_size), "member": lax.rem(d, group_size)}

    loads = [
        pltpu.make_async_copy(src, dst, local_sem.at[i])
        for i, (src, dst) in enumerate(
            [
                (memory, mem),
                (msg_w, msg_v),
                (st_w, st_v),
                (in_w, in_v),
                (q_w, q_v),
                (k_w, k_v),
                (v_w, v_v),
                (m_w, m_v),
            ]
        )
    ]
    for load in loads:
        load.start()

    def greet(t, _):
        _, dev = device(t + 1)
        pl.semaphore_signal(barrier, inc=1, device_id=dev, device_id_type=MESH)
        return 0

    lax.fori_loop(0, device_count - 1, greet, 0)

    places_row, places_col = [], []
    for role, owner_ref in enumerate((s_owner, t_owner)):
        own_row = owner_ref[...].astype(F32)
        own_col = column(own_row)
        same = own_col == own_row
        up = iota((events, events), 0) < iota((events, events), 1)
        down = iota((events, events), 1) < iota((events, events), 0)
        rank_row = jnp.sum(jnp.where(same & up, 1.0, 0.0), axis=0, keepdims=True)
        rank_col = jnp.sum(jnp.where(same & down, 1.0, 0.0), axis=1, keepdims=True)
        places_row.append(own_row * 8.0 + (rank_row + 4.0 * role))
        places_col.append(own_col * 8.0 + (rank_col + 4.0 * role))
    place_row = jnp.concatenate(places_row, axis=1).astype(I32)
    wanted_row = jnp.concatenate([s_row[...], t_row[...]], axis=1).astype(F32) + 1.0

    def request(j, _):
        base = j * LANES
        hit = place_row == iota((LANES, 2 * events), 0) + base
        asked = jnp.sum(jnp.where(hit, wanted_row, 0.0), axis=1, keepdims=True) - 1.0
        asked = jnp.broadcast_to(asked, (LANES, LANES)).astype(I32)
        req_out[pl.ds(j * 16, 16)] = asked.reshape(16, 8, LANES)
        return 0

    lax.fori_loop(0, slots // LANES, request, 0)

    pl.semaphore_wait(barrier, device_count - 1)

    def exchange_one(src, dst, t, sem):
        d, dev = device(t)
        pltpu.make_async_remote_copy(
            src_ref=src.at[d],
            dst_ref=dst.at[me],
            send_sem=send_sem.at[sem],
            recv_sem=recv_sem.at[sem],
            device_id=dev,
            device_id_type=MESH,
        ).start()

    def exchange_wait(src, dst, sem):
        part = dst.at[pl.ds(0, device_count - 1)]
        pltpu.make_async_copy(part, part, recv_sem.at[sem]).wait()
        part = src.at[pl.ds(0, device_count - 1)]
        pltpu.make_async_copy(part, part, send_sem.at[sem]).wait()

    def send_request(t, _):
        exchange_one(req_out, req_in, t + 1, 0)
        return 0

    lax.fori_loop(0, device_count - 1, send_request, 0)
    req_in[me] = req_out[me]

    loads[0].wait()

    def split(j, _):
        rows = pl.ds(j * LANES, LANES)
        x = mem[rows, :]
        hi = x.astype(BF16)
        mem_hi[rows, :] = hi
        mem_lo[rows, :] = (x - hi.astype(F32)).astype(BF16)
        return 0

    lax.fori_loop(0, nodes // LANES, split, 0)

    exchange_wait(req_out, req_in, 0)

    chunk = 2 * LANES
    peers = chunk // 8

    def chunk_of(j):
        return lax.rem(lax.div(me, peers) + j, device_count // peers)

    def send_chunk(src, dst, j, sem):
        first = chunk_of(j) * peers

        def one(i, _):
            d = first + lax.rem(lax.rem(me, peers) + i, peers)

            @pl.when(d != me)
            def _():
                exchange_one(src, dst, d - me + device_count, sem)

            return 0

        lax.fori_loop(0, peers, one, 0)

    def serve(j, _):
        c = chunk_of(j)
        asked = req_in[pl.ds(c * peers, peers)].reshape(chunk, LANES)
        lane = iota((chunk, LANES), 1)
        hot = [
            jnp.where(asked == lane + b * LANES, 1.0, 0.0).astype(BF16)
            for b in range(nodes // LANES)
        ]
        rows = dot(jnp.concatenate(hot, axis=1), mem_hi[...])
        xout[pl.ds(c * peers, peers)] = rows.reshape(peers, 8, width).astype(BF16)
        send_chunk(xout, fetched, j, 1)
        return 0

    lax.fori_loop(0, slots // chunk, serve, 0)
    fetched[me] = xout[me]

    lane_slots = iota((events, slots), 1)
    for role in range(2):
        hit = lane_slots == places_col[role].astype(I32)
        pick[pl.ds(role * events, events), :] = jnp.where(hit, 1.0, 0.0).astype(BF16)

    def placing(j, _):
        hit = place_row == iota((LANES, 2 * events), 0) + j * LANES
        place[pl.ds(j * LANES, LANES), :] = jnp.where(hit, 1.0, 0.0).astype(BF16)
        return 0

    lax.fori_loop(0, slots // LANES, placing, 0)

    time_col = column(e_time[...].astype(F32))
    stamp = cosine(time_col * freq[...] + phase[...]).astype(BF16)
    for load in loads[1:]:
        load.wait()
    stamped = dot(stamp, msg_v[pl.ds(2 * width, LANES), :]) + msg_b[...]

    for b in range(slots // LANES):
        asked = req_in[pl.ds(b * 16, 16)].reshape(LANES, LANES)
        diagonal = iota((LANES, LANES), 0) == iota((LANES, LANES), 1)
        slot_row[:, pl.ds(b * LANES, LANES)] = jnp.sum(
            jnp.where(diagonal, asked.astype(F32), 0.0), axis=0, keepdims=True
        )

    def back_matrix(j, _):
        rows = pl.ds(j * LANES, LANES)
        node = (iota((LANES, slots), 0) + j * LANES).astype(F32)
        hot = jnp.where(slot_row[...] == node, 1.0, 0.0)
        back[rows, :] = hot.astype(BF16)
        touched[rows, :] = jnp.broadcast_to(
            jnp.sum(hot, axis=1, keepdims=True), (LANES, LANES)
        )
        return 0

    lax.fori_loop(0, nodes // LANES, back_matrix, 0)

    exchange_wait(xout, fetched, 1)

    rows_in = fetched[...].reshape(slots, width)
    for role in range(2):
        msgs[pl.ds(role * events, events), :] = dot(
            pick[pl.ds(role * events, events), :], rows_in
        ).astype(BF16)
    source_mem = msgs[pl.ds(0, events), :]
    target_mem = msgs[pl.ds(events, events), :]
    first_w = msg_v[pl.ds(0, width), :]
    second_w = msg_v[pl.ds(width, width), :]
    to_source = dot(source_mem, first_w) + dot(target_mem, second_w) + stamped
    to_target = dot(target_mem, first_w) + dot(source_mem, second_w) + stamped
    msgs[pl.ds(0, events), :] = jnp.maximum(to_source, 0.0).astype(BF16)
    msgs[pl.ds(events, events), :] = jnp.maximum(to_target, 0.0).astype(BF16)

    def give_back(j, _):
        c = chunk_of(j)
        rows = dot(place[pl.ds(c * chunk, chunk), :], msgs[...])
        yout[pl.ds(c * peers, peers)] = rows.reshape(peers, 8, width).astype(BF16)
        send_chunk(yout, inbound, j, 2)
        return 0

    lax.fori_loop(0, slots // chunk, give_back, 0)
    inbound[me] = yout[me]

    query_col = column(q_rows[...].astype(F32))
    query_hot = jnp.where(
        iota((queries, nodes), 1).astype(F32) == query_col, 1.0, 0.0
    ).astype(BF16)
    query_slots = jnp.where(slot_row[...] == query_col, 1.0, 0.0)
    query_touched = jnp.sum(query_slots, axis=1, keepdims=True)
    query_slots = query_slots.astype(BF16)
    query_hi = dot(query_hot, mem_hi[...])
    query_mem = query_hi + dot(query_hot, mem_lo[...])
    query_state = dot(query_hi.astype(BF16), st_v[...]) + st_b[...]

    links = l_slot.shape[1]
    link_id = iota((queries, links), 1)
    first_link = iota((queries, links), 0) * FAN
    mine = (link_id >= first_link) & (link_id < first_link + FAN)
    link_f = iota((links, LANES), 0).astype(F32)
    link_k = link_f - FAN * jnp.floor((link_f + 0.5) * (1.0 / FAN))
    spread = jnp.where(link_k == iota((links, LANES), 1).astype(F32), 1.0, 0.0).astype(BF16)

    def arranged(row):
        return dot(jnp.where(mine, row.astype(F32), 0.0).astype(BF16), spread)

    lane_q = iota((queries, LANES), 1)
    live = lane_q < FAN
    slot_f = arranged(l_slot[...])
    member_f = arranged(l_member[...])
    high = jnp.right_shift(l_delta[...], 4)
    delta_f = arranged(high) * 16.0 + arranged(l_delta[...] - high * 16)
    slot_i = jnp.where(live, slot_f, 0.0).astype(I32)
    member_i = jnp.where(live, member_f, -1.0).astype(I32)
    link_i = member_i * LANES + slot_i

    for k in range(FAN):
        code[k] = cosine(delta_f[:, k : k + 1] * freq[...] + phase[...]).astype(BF16)
    self_code = cosine(phase[...]).astype(BF16)

    def invert(b, _):
        node = lane_q + b * LANES
        found = jnp.full((queries, LANES), LANES - 1, I32)
        for k in range(FAN):
            found = jnp.where(link_i[:, k : k + 1] == node, k, found)
        inverse[b] = found
        return 0

    lax.fori_loop(0, group_size, invert, 0)

    def states(j, _):
        rows = pl.ds(j * chunk, chunk)
        state[rows, :] = dot(mem_hi[rows, :], st_v[...]) + st_b[...]
        return 0

    lax.fori_loop(0, nodes // chunk, states, 0)

    exchange_wait(yout, inbound, 2)

    def cell(mean_msg, old, from_state):
        def part(i):
            return dot(mean_msg, in_v[:, i * width : (i + 1) * width]) + in_b[:, i * width : (i + 1) * width]

        reset = jax.nn.sigmoid(part(0) + from_state[:, :width])
        update = jax.nn.sigmoid(part(1) + from_state[:, width : 2 * width])
        candidate = jnp.tanh(part(2) + reset * from_state[:, 2 * width :])
        return (1.0 - update) * candidate + update * old

    messages_in = inbound[...].reshape(slots, width)
    query_mean = (dot(query_slots, messages_in) / jnp.maximum(query_touched, 1.0)).astype(BF16)
    fresh = cell(query_mean, query_mem, query_state)
    feats = jnp.where(query_touched > 0.0, fresh, query_mem).astype(BF16)

    def refresh(j, _):
        rows = pl.ds(j * LANES, LANES)
        count = touched[rows, 0:1]
        mean = dot(back[rows, :], inbound[...].reshape(slots, width)) / jnp.maximum(count, 1.0)
        old = mem[rows, :]
        new = cell(mean.astype(BF16), old, state[rows, :])
        mem[rows, :] = jnp.where(count > 0.0, new, old)
        return 0

    parity = lax.rem(member, 2)
    first_stride = 2 + 6 * parity
    second_stride = 8 - 6 * parity
    a_pos = lax.rem(lax.div(member, first_stride), 4)
    b_pos = lax.rem(lax.div(member, second_stride), 4)

    def at(da, db):
        return (
            lax.rem(a_pos + da + 4, 4) * first_stride
            + lax.rem(b_pos + db + 4, 4) * second_stride
            + parity
        )

    sibling = member + 1 - 2 * parity
    half = queries // 2

    for hop in range(2):
        rows_of = table.at[hop]
        sends = hop_send.at[hop]
        arrivals = hop_recv.at[hop]

        def piece(ref, which):
            return ref if which is None else ref.at[pl.ds(which * half, half)]

        def send(block, to, which=None):
            part = piece(rows_of.at[block], which)
            pltpu.make_async_remote_copy(
                src_ref=part,
                dst_ref=part,
                send_sem=sends,
                recv_sem=arrivals.at[block, 1 if which == 1 else 0],
                device_id={"member": to},
                device_id_type=MESH,
            ).start()

        def arrive(block, which=None):
            part = piece(rows_of.at[block], which)
            pltpu.make_async_copy(part, part, arrivals.at[block, 1 if which == 1 else 0]).wait()

        a_next, a_last, b_next, b_last = at(1, 0), at(-1, 0), at(0, 1), at(0, -1)

        rows_of[member] = feats
        for to in (a_next, a_last, b_next, b_last, sibling):
            send(member, to)

        query_w = q_v.at[hop]
        key_w = k_v.at[hop]
        merge_w = m_v.at[hop]
        query_vec = dot(feats, query_w[pl.ds(0, width), :]) + dot(
            jnp.broadcast_to(self_code, (8, LANES)), query_w[pl.ds(width, LANES), :]
        )[0:1]
        merged_self = dot(feats, merge_w[pl.ds(width, width), :]) + m_b[hop : hop + 1, :]
        head = width // HEADS
        for h in range(HEADS):
            u = dot_t(
                (query_vec[:, h * head : (h + 1) * head] * (1.0 / math.sqrt(head))).astype(BF16),
                key_w[:, h * head : (h + 1) * head],
            )
            u_buf[pl.ds(h * queries, queries), :] = u[:, :width].astype(BF16)
            u_code = u[:, width:]
            c = jnp.full((queries, LANES), NEG, F32)
            for k in range(FAN):
                c = jnp.where(
                    lane_q == k,
                    jnp.sum(u_code * code[k].astype(F32), axis=1, keepdims=True),
                    c,
                )
            most = c
            for k in range(FAN):
                alike = (link_i == link_i[:, k : k + 1]) & live
                most = jnp.where(alike, jnp.maximum(most, c[:, k : k + 1]), most)
            total = jnp.zeros((queries, LANES), F32)
            for k in range(FAN):
                alike = (link_i == link_i[:, k : k + 1]) & live
                total = total + jnp.where(alike, jnp.exp(c[:, k : k + 1] - most), 0.0)
            cp[h] = jnp.where(live, most + jnp.log(jnp.where(live, total, 1.0)), NEG)
            cp[HEADS + h] = c
            s_acc[h] = jnp.zeros((queries, LANES), F32)
        acc[...] = jnp.zeros_like(acc)

        def attend(da, db):
            chip = lax.div(at(da, db), 2)
            arrive(2 * chip + 1 - parity)
            rows = rows_of[pl.ds(2 * chip, 2)].reshape(2 * queries, width)
            scores = dot_t(u_buf[...], rows)
            parts = []
            for h in range(HEADS):
                sides = []
                for side in range(2):
                    s = scores[
                        h * queries : (h + 1) * queries, side * queries : (side + 1) * queries
                    ]
                    bias = jnp.take_along_axis(cp[h], inverse[2 * chip + side], axis=1)
                    sides.append(jnp.exp(s + bias).astype(BF16))
                    picked = jnp.take_along_axis(s, slot_i, axis=1)
                    s_acc[h] = jnp.where(member_i == 2 * chip + side, picked, s_acc[h])
                parts.append(jnp.concatenate(sides, axis=1))
            acc[...] += dot(jnp.concatenate(parts, axis=0), rows)

        if hop == 0:
            lax.fori_loop(0, 4, refresh, 0)

        arrive(at(-1, 0))
        send(at(-1, 0), a_next, 0)
        for to in (b_next, b_last, sibling):
            send(at(-1, 0), to)
        arrive(at(1, 0))
        send(at(1, 0), a_last, 1)
        for to in (b_next, b_last, sibling):
            send(at(1, 0), to)
        arrive(at(0, -1))
        send(at(0, -1), b_next, 0)
        send(at(0, -1), sibling)
        arrive(at(0, 1))
        send(at(0, 1), b_last, 1)
        send(at(0, 1), sibling)
        attend(0, 0)
        for which in range(2):
            arrive(at(2, 0), which)
        for to in (b_next, b_last, sibling):
            send(at(2, 0), to)
        for which in range(2):
            arrive(at(0, 2), which)
        send(at(0, 2), sibling)
        if hop == 0:
            lax.fori_loop(4, 8, refresh, 0)
        for da, db in ((-1, 0), (1, 0), (0, -1), (0, 1)):
            attend(da, db)
        for da in (-1, 1):
            for db in (-1, 1):
                arrive(at(da, db))
                send(at(da, db), b_next if db == -1 else b_last, 0 if db == -1 else 1)
                send(at(da, db), sibling)
        attend(2, 0)
        attend(0, 2)
        for db in (-1, 1):
            arrive(at(2, db))
            send(at(2, db), b_next if db == -1 else b_last, 0 if db == -1 else 1)
            send(at(2, db), sibling)
        for da in (-1, 1):
            for which in range(2):
                arrive(at(da, 2), which)
            send(at(da, 2), sibling)
        for da in (-1, 1):
            for db in (-1, 1):
                attend(da, db)
        for which in range(2):
            arrive(at(2, 2), which)
        send(at(2, 2), sibling)
        for da, db in ((2, -1), (2, 1), (-1, 2), (1, 2)):
            attend(da, db)
        if hop == 0:
            store = pltpu.make_async_copy(mem, new_memory, out_sem)
            store.start()
        attend(2, 2)

        value_w = v_v.at[hop]
        mixed = []
        for h in range(HEADS):
            w = jnp.where(live, jnp.exp(s_acc[h] + cp[HEADS + h]), 0.0)
            scale = 1.0 / jnp.sum(w, axis=1, keepdims=True)
            w = w * scale
            coded = jnp.zeros((queries, LANES), F32)
            for k in range(FAN):
                coded = coded + w[:, k : k + 1] * code[k].astype(F32)
            rows = (acc[pl.ds(h * queries, queries), :] * scale).astype(BF16)
            cols = slice(h * head, (h + 1) * head)
            mixed.append(
                dot(rows, value_w[pl.ds(0, width), cols])
                + dot(coded.astype(BF16), value_w[pl.ds(width, LANES), cols])
            )
        mixed = jnp.concatenate(mixed, axis=1).astype(BF16)
        merged = dot(mixed, merge_w[pl.ds(0, width), :]) + merged_self
        feats = jnp.maximum(merged, 0.0).astype(BF16)

        whole = rows_of.at[pl.ds(0, group_size - 1)]
        pltpu.make_async_copy(whole, whole, sends).wait()

    embedding[...] = feats
    store.wait()


def on_device(
    memory,
    source_owner,
    target_owner,
    source_row,
    target_row,
    event_time,
    query_rows,
    link_member,
    link_slot,
    link_delta,
    frequency,
    time_phase,
    msg_weight,
    msg_bias,
    input_weight,
    state_weight,
    input_bias,
    state_bias,
    query_weight,
    key_weight,
    value_weight,
    merge_weight,
    merge_bias,
):
    device_count = lax.axis_size(("group", "member"))
    group_size = lax.axis_size("member")
    nodes, width = memory.shape
    events = source_row.shape[0]
    queries = query_rows.shape[0]
    slots = device_count * 8

    def flat(x):
        return x.reshape(1, -1)

    vmem = pl.BlockSpec(memory_space=pltpu.VMEM)
    hbm = pl.BlockSpec(memory_space=pl.ANY)
    return pl.pallas_call(
        functools.partial(kernel, group_size, device_count),
        out_shape=(
            jax.ShapeDtypeStruct((nodes, width), F32),
            jax.ShapeDtypeStruct((queries, width), BF16),
        ),
        in_specs=[hbm] + [vmem] * 11 + [hbm, vmem, hbm, hbm, vmem, vmem] + [hbm] * 4 + [vmem],
        out_specs=(hbm, vmem),
        scratch_shapes=[
            pltpu.VMEM((nodes, width), F32),
            pltpu.VMEM((nodes, width), BF16),
            pltpu.VMEM((nodes, width), BF16),
            pltpu.VMEM(msg_weight.shape, BF16),
            pltpu.VMEM(input_weight.shape, BF16),
            pltpu.VMEM(state_weight.shape, BF16),
            pltpu.VMEM(query_weight.shape, BF16),
            pltpu.VMEM(key_weight.shape, BF16),
            pltpu.VMEM(value_weight.shape, BF16),
            pltpu.VMEM(merge_weight.shape, BF16),
            pltpu.VMEM((device_count, 8, LANES), I32),
            pltpu.VMEM((device_count, 8, LANES), I32),
            pltpu.VMEM((1, slots), F32),
            pltpu.VMEM((device_count, 8, width), BF16),
            pltpu.VMEM((device_count, 8, width), BF16),
            pltpu.VMEM((device_count, 8, width), BF16),
            pltpu.VMEM((device_count, 8, width), BF16),
            pltpu.VMEM((2 * events, slots), BF16),
            pltpu.VMEM((slots, 2 * events), BF16),
            pltpu.VMEM((2 * events, width), BF16),
            pltpu.VMEM((nodes, slots), BF16),
            pltpu.VMEM((nodes, LANES), F32),
            pltpu.VMEM((nodes, 3 * width), F32),
            pltpu.VMEM((2, group_size, queries, width), BF16),
            pltpu.VMEM((group_size, queries, LANES), I32),
            pltpu.VMEM((FAN, queries, LANES), BF16),
            pltpu.VMEM((HEADS * queries, width), BF16),
            pltpu.VMEM((2 * HEADS, queries, LANES), F32),
            pltpu.VMEM((HEADS, queries, LANES), F32),
            pltpu.VMEM((HEADS * queries, width), F32),
            pltpu.SemaphoreType.DMA((8,)),
            pltpu.SemaphoreType.DMA,
            pltpu.SemaphoreType.DMA((3,)),
            pltpu.SemaphoreType.DMA((3,)),
            pltpu.SemaphoreType.DMA((2,)),
            pltpu.SemaphoreType.DMA((2, group_size, 2)),
        ],
        compiler_params=pltpu.CompilerParams(
            collective_id=0, has_side_effects=True, vmem_limit_bytes=56 * 2**20
        ),
    )(
        memory,
        flat(source_owner),
        flat(target_owner),
        flat(source_row),
        flat(target_row),
        flat(event_time),
        flat(query_rows),
        flat(link_member),
        flat(link_slot),
        flat(link_delta),
        flat(frequency),
        flat(time_phase),
        msg_weight,
        flat(msg_bias),
        input_weight,
        state_weight,
        flat(input_bias),
        flat(state_bias),
        query_weight,
        key_weight,
        value_weight,
        merge_weight,
        merge_bias,
    )


def solution(mesh):
    both = ("group", "member")
    rows = P(both, None)
    flat = P(both)
    in_specs = (rows,) * 3 + (flat,) * 4 + (rows,) + (flat,) * 2 + (P(),) * 13
    return jax.shard_map(
        on_device, mesh=mesh, in_specs=in_specs, out_specs=(rows, rows), check_vma=False
    )
```

time: 253 us -> 120 us (0.47)
  Pallas kernels: 0 us -> 110 us
  local copies, waits for them, and re-layouts: 78.5 us -> 8.95 us
  waiting for transfers between devices: 68.4 us -> 0 us
  starting transfers between devices: 45.6 us -> 0 us
  other arithmetic: 35.9 us -> 0 us
  matrix products: 20.7 us -> 0 us
    pallas_call x0 -> x1, Pallas kernels: none -> 110 us  [on_device(): pl.pallas_call(functools.partial(kernel, group_size, device_count), out_s...]
    all_to_all x6 -> x0, waiting for transfers between devices: 68.4 us -> none  [the longest x2 49 us: fetch_rows(): lax.all_to_all(feature_rows[served_rows].reshape(member_count, room_each,...]
    all_to_all x6 -> x0, starting transfers between devices: 45.6 us -> none  [the longest x2 12.6 us: fetch_rows(): lax.all_to_all(feature_rows[served_rows].reshape(member_count, room_each,...]
    gather x8 -> x0, local copies, waits for them, and re-layouts: 40.4 us -> none  [the longest x2 16.4 us: fetch_rows(): feature_rows[served_rows].reshape(member_count, room_each, row_width)]
    dot_general x11 -> x0, matrix products: 20.7 us -> none  [the longest x1 6.05 us: gru_cell(): jnp.dot(hidden.astype(jnp.bfloat16), state_weight, preferred_element_type...]
    scatter-add x2 -> x0, other arithmetic: 14.1 us -> none  [the longest x1 8.15 us: on_device(): jax.ops.segment_sum(inbound.astype(jnp.float32), target_rows, num_segment...]
    dot_general x9 -> x0, local copies, waits for them, and re-layouts: 13.5 us -> none  [the longest x3 5.48 us: attend(): jnp.dot(key_input, value_weight, preferred_element_type=jnp.float32)]
    scatter x3 -> x0, local copies, waits for them, and re-layouts: 11.3 us -> none  [the longest x1 5.42 us: on_device(): jnp.full((member_count * room_each,), -1, jnp.int32).at[spot_index]]
  transfers between devices with their start and end apart: 6 -> 0, of which waited for: 4 -> 0; matrix products, arithmetic and copies ran while one was open for 22% -> 0% of each run, Pallas kernels for 0% -> 0%
where the time goes in v1:
time: 120 us
  Pallas kernels  110 us (92%)
  local copies, waits for them, and re-layouts  8.95 us (7%)
    pallas_call x1, Pallas kernels, on_device(): pl.pallas_call(functools.partial(kernel, group_size, device_count), out_s...  110 us
    reshape x4, local copies, waits for them, and re-layouts, flat(): return x.reshape(1, -1)  5.18 us
    unnamed x4, local copies, waits for them, and re-layouts  3.77 us

profile of v1, /device:TPU:1, one launch (start us, length us, event | category | flops | bytes accessed | tf_op | source)
XLA Modules:
  0.0 119.9 jit_solution(14336952697141811175)
XLA Ops:
  0.6 1.3 %reshape.53.l_slot = s32[1,1280]{1,0:T(1,128)} reshape(s32[1280]{0:T(1024)} %param.31) | data formatting | bytes 10240 | tf_op jit(solution)/shard_map/reshape | solution.py:609
  1.9 1.3 %reshape.54.l_delta = s32[1,1280]{1,0:T(1,128)} reshape(s32[1280]{0:T(1024)} %param.32) | data formatting | bytes 10240 | tf_op jit(solution)/shard_map/reshape | solution.py:609
  3.2 1.3 %reshape.58.in_b = f32[1,1536]{1,0:T(1,128)} reshape(f32[1536]{0:T(1024)} %param.39) | data formatting | bytes 12288 | tf_op jit(solution)/shard_map/reshape | solution.py:609
  4.5 1.3 %reshape.59.st_b = f32[1,1536]{1,0:T(1,128)} reshape(f32[1536]{0:T(1024)} %param.40) | data formatting | bytes 12288 | tf_op jit(solution)/shard_map/reshape | solution.py:609
  5.8 110.3 %shard_map.230 = (f32[1024,512]{1,0:T(8,128)}, bf16[128,512]{1,0:T(8,128)(2,1)}) custom-call(f32[1024,512]{1,0:T(8,128)} %memory.1, s32[1,256]{1,0:T(1,128)} %bitcast.12, s32[1,256]{1,0:T(1,128)} %bitcast.13, s32[1,256]{1,0:T(1,128)} %bitcast.14, s32[1,256]{1,0:T(1,128)} %bitcast.15, s32[1,256]{1,0:T(1,128)} %bitcast.16, s32[1,128]{1,0:T(1,128)} %bitcast.17, ...), custom_call_target="tpu_custom_call" | custom-call | tf_op jit(solution)/shard_map/pallas_call | solution.py:613
  116.1 0.0 copy-start
  116.1 3.1 %copy.27 = f32[1024,512]{1,0:T(8,128)} copy(f32[1024,512]{1,0:T(8,128)} %get-tuple-element.4) | data formatting | bytes 4194304
  119.2 0.0 copy-done
  119.2 0.7 copy.28
Async XLA Ops:
  116.1 3.1 %copy-start = (bf16[128,512]{1,0:T(8,128)(2,1)S(1)}, bf16[128,512]{1,0:T(8,128)(2,1)}, u32[]{:S(2)}) copy-start(bf16[128,512]{1,0:T(8,128)(2,1)} %get-tuple-element.5) | copy-start | bytes 393220

commit v2 on v1

--- a/solution.py
+++ b/solution.py
@@ -45,6 +45,10 @@
 def column(row):
     n = row.shape[1]
     return jnp.sum(jnp.where(iota((n, n), 0) == iota((n, n), 1), row, 0.0), axis=1, keepdims=True)
+
+
+def lanes_row(ref):
+    return jnp.concatenate([ref[i : i + 1, :] for i in range(ref.shape[0])], axis=1)
 
 
 def kernel(
@@ -75,7 +79,6 @@
     m_b,
     new_memory,
     embedding,
-    mem,
     mem_hi,
     mem_lo,
     msg_v,
@@ -87,6 +90,7 @@
     m_v,
     req_out,
     req_in,
+    req_rows,
     slot_row,
     xout,
     fetched,
@@ -112,14 +116,29 @@
     hop_send,
     hop_recv,
 ):
+    mem = new_memory
     group = lax.axis_index("group")
     member = lax.axis_index("member")
     me = group * group_size + member
     nodes, width = mem.shape
+    in_bias = lanes_row(in_b)
+    st_bias = lanes_row(st_b)
     events = s_row.shape[1]
     queries = q_rows.shape[1]
     slots = device_count * 8
     barrier = pltpu.get_barrier_semaphore()
+
+    x_pos = lax.rem(lax.div(member, 2), 4)
+    z_pos = lax.div(member, 8)
+    core = lax.rem(member, 2)
+    batch = lax.rem(group + z_pos + x_pos, 4)
+    place_me = batch * 32 + group * 8 + z_pos * 2 + core
+
+    def position(owner):
+        y = jnp.right_shift(owner, 5)
+        z = jnp.bitwise_and(jnp.right_shift(owner, 3), 3)
+        x = jnp.bitwise_and(jnp.right_shift(owner, 1), 3)
+        return jnp.bitwise_and(x + y + z, 3) * 32 + y * 8 + z * 2 + jnp.bitwise_and(owner, 1)
 
     def device(t):
         d = lax.rem(me + t, device_count)
@@ -152,7 +171,7 @@
 
     places_row, places_col = [], []
     for role, owner_ref in enumerate((s_owner, t_owner)):
-        own_row = owner_ref[...].astype(F32)
+        own_row = position(owner_ref[...]).astype(F32)
         own_col = column(own_row)
         same = own_col == own_row
         up = iota((events, events), 0) < iota((events, events), 1)
@@ -164,28 +183,41 @@
     place_row = jnp.concatenate(places_row, axis=1).astype(I32)
     wanted_row = jnp.concatenate([s_row[...], t_row[...]], axis=1).astype(F32) + 1.0
 
-    def request(j, _):
-        base = j * LANES
-        hit = place_row == iota((LANES, 2 * events), 0) + base
-        asked = jnp.sum(jnp.where(hit, wanted_row, 0.0), axis=1, keepdims=True) - 1.0
-        asked = jnp.broadcast_to(asked, (LANES, LANES)).astype(I32)
-        req_out[pl.ds(j * 16, 16)] = asked.reshape(16, 8, LANES)
-        return 0
-
-    lax.fori_loop(0, slots // LANES, request, 0)
+    lane_d = iota((device_count, LANES), 1)
+    asked_out = jnp.zeros((device_count, LANES), F32)
+    for slot in range(8):
+        role_lanes = slice(0, events) if slot < 4 else slice(events, 2 * events)
+        hit = place_row[:, role_lanes] == iota((device_count, events), 0) * 8 + slot
+        asked = jnp.sum(jnp.where(hit, wanted_row[:, role_lanes], 0.0), axis=1, keepdims=True)
+        asked_out = jnp.where(lane_d == slot, asked - 1.0, asked_out)
+    req_out[:, 0, :] = asked_out.astype(I32)
 
     pl.semaphore_wait(barrier, device_count - 1)
 
-    def exchange_one(src, dst, t, sem):
-        d, dev = device(t)
-        pltpu.make_async_remote_copy(
-            src_ref=src.at[d],
-            dst_ref=dst.at[me],
-            send_sem=send_sem.at[sem],
-            recv_sem=recv_sem.at[sem],
-            device_id=dev,
-            device_id_type=MESH,
-        ).start()
+    def exchange(src, dst, j, sem):
+        def one(i, _):
+            q = lax.rem(lax.rem(i, 16) * 7, 16)
+            y = lax.rem(group + lax.div(q, 4), 4)
+            z = lax.rem(z_pos + lax.rem(q, 4), 4)
+            c = lax.rem(core + i + lax.div(i, 16), 2)
+            k = lax.rem(batch + j, 4)
+            x = lax.rem(k - y - z + 8, 4)
+            place = k * 32 + y * 8 + z * 2 + c
+
+            @pl.when(place != place_me)
+            def _():
+                pltpu.make_async_remote_copy(
+                    src_ref=src.at[place],
+                    dst_ref=dst.at[place_me],
+                    send_sem=send_sem.at[sem],
+                    recv_sem=recv_sem.at[sem],
+                    device_id={"group": y, "member": z * 8 + x * 2 + c},
+                    device_id_type=MESH,
+                ).start()
+
+            return 0
+
+        lax.fori_loop(0, 32, one, 0)
 
     def exchange_wait(src, dst, sem):
         part = dst.at[pl.ds(0, device_count - 1)]
@@ -193,12 +225,12 @@
         part = src.at[pl.ds(0, device_count - 1)]
         pltpu.make_async_copy(part, part, send_sem.at[sem]).wait()
 
-    def send_request(t, _):
-        exchange_one(req_out, req_in, t + 1, 0)
-        return 0
-
-    lax.fori_loop(0, device_count - 1, send_request, 0)
-    req_in[me] = req_out[me]
+    def send_requests(j, _):
+        exchange(req_out, req_in, j + 1, 0)
+        return 0
+
+    lax.fori_loop(0, 4, send_requests, 0)
+    req_in[place_me] = req_out[place_me]
 
     loads[0].wait()
 
@@ -216,39 +248,30 @@
 
     chunk = 2 * LANES
     peers = chunk // 8
-
-    def chunk_of(j):
-        return lax.rem(lax.div(me, peers) + j, device_count // peers)
-
-    def send_chunk(src, dst, j, sem):
-        first = chunk_of(j) * peers
-
-        def one(i, _):
-            d = first + lax.rem(lax.rem(me, peers) + i, peers)
-
-            @pl.when(d != me)
-            def _():
-                exchange_one(src, dst, d - me + device_count, sem)
-
-            return 0
-
-        lax.fori_loop(0, peers, one, 0)
+    req_rows[...] = req_in[:, 0, :]
+
+    def asked_column(first, count):
+        part = req_rows[pl.ds(first, count), :].astype(F32)
+        spread_out = jnp.broadcast_to(part[:, None, :], (count, 8, LANES))
+        mine_of = iota((count, 8, LANES), 1) == iota((count, 8, LANES), 2)
+        column_of = jnp.sum(jnp.where(mine_of, spread_out, 0.0), axis=2, keepdims=True)
+        return column_of.reshape(count * 8, 1)
 
     def serve(j, _):
-        c = chunk_of(j)
-        asked = req_in[pl.ds(c * peers, peers)].reshape(chunk, LANES)
-        lane = iota((chunk, LANES), 1)
+        c = lax.rem(batch + j + 1, 4)
+        asked = asked_column(pl.multiple_of(c * peers, peers), peers)
+        lane = iota((chunk, LANES), 1).astype(F32)
         hot = [
-            jnp.where(asked == lane + b * LANES, 1.0, 0.0).astype(BF16)
+            jnp.where(asked == lane + float(b * LANES), 1.0, 0.0).astype(BF16)
             for b in range(nodes // LANES)
         ]
         rows = dot(jnp.concatenate(hot, axis=1), mem_hi[...])
         xout[pl.ds(c * peers, peers)] = rows.reshape(peers, 8, width).astype(BF16)
-        send_chunk(xout, fetched, j, 1)
+        exchange(xout, fetched, j + 1, 1)
         return 0
 
     lax.fori_loop(0, slots // chunk, serve, 0)
-    fetched[me] = xout[me]
+    fetched[place_me] = xout[place_me]
 
     lane_slots = iota((events, slots), 1)
     for role in range(2):
@@ -269,10 +292,10 @@
     stamped = dot(stamp, msg_v[pl.ds(2 * width, LANES), :]) + msg_b[...]
 
     for b in range(slots // LANES):
-        asked = req_in[pl.ds(b * 16, 16)].reshape(LANES, LANES)
+        asked = asked_column(b * 16, 16)
         diagonal = iota((LANES, LANES), 0) == iota((LANES, LANES), 1)
         slot_row[:, pl.ds(b * LANES, LANES)] = jnp.sum(
-            jnp.where(diagonal, asked.astype(F32), 0.0), axis=0, keepdims=True
+            jnp.where(diagonal, asked, 0.0), axis=0, keepdims=True
         )
 
     def back_matrix(j, _):
@@ -304,14 +327,14 @@
     msgs[pl.ds(events, events), :] = jnp.maximum(to_target, 0.0).astype(BF16)
 
     def give_back(j, _):
-        c = chunk_of(j)
+        c = lax.rem(batch + j + 1, 4)
         rows = dot(place[pl.ds(c * chunk, chunk), :], msgs[...])
         yout[pl.ds(c * peers, peers)] = rows.reshape(peers, 8, width).astype(BF16)
-        send_chunk(yout, inbound, j, 2)
+        exchange(yout, inbound, j + 1, 2)
         return 0
 
     lax.fori_loop(0, slots // chunk, give_back, 0)
-    inbound[me] = yout[me]
+    inbound[place_me] = yout[place_me]
 
     query_col = column(q_rows[...].astype(F32))
     query_hot = jnp.where(
@@ -322,9 +345,12 @@
     query_slots = query_slots.astype(BF16)
     query_hi = dot(query_hot, mem_hi[...])
     query_mem = query_hi + dot(query_hot, mem_lo[...])
-    query_state = dot(query_hi.astype(BF16), st_v[...]) + st_b[...]
-
-    links = l_slot.shape[1]
+    query_state = dot(query_hi.astype(BF16), st_v[...]) + st_bias
+
+    slot_of = lanes_row(l_slot)
+    delta_of = lanes_row(l_delta)
+    member_of = l_member[...]
+    links = slot_of.shape[1]
     link_id = iota((queries, links), 1)
     first_link = iota((queries, links), 0) * FAN
     mine = (link_id >= first_link) & (link_id < first_link + FAN)
@@ -337,10 +363,10 @@
 
     lane_q = iota((queries, LANES), 1)
     live = lane_q < FAN
-    slot_f = arranged(l_slot[...])
-    member_f = arranged(l_member[...])
-    high = jnp.right_shift(l_delta[...], 4)
-    delta_f = arranged(high) * 16.0 + arranged(l_delta[...] - high * 16)
+    slot_f = arranged(slot_of)
+    member_f = arranged(member_of)
+    high = jnp.right_shift(delta_of, 4)
+    delta_f = arranged(high) * 16.0 + arranged(delta_of - high * 16)
     slot_i = jnp.where(live, slot_f, 0.0).astype(I32)
     member_i = jnp.where(live, member_f, -1.0).astype(I32)
     link_i = member_i * LANES + slot_i
@@ -361,7 +387,7 @@
 
     def states(j, _):
         rows = pl.ds(j * chunk, chunk)
-        state[rows, :] = dot(mem_hi[rows, :], st_v[...]) + st_b[...]
+        state[rows, :] = dot(mem_hi[rows, :], st_v[...]) + st_bias
         return 0
 
     lax.fori_loop(0, nodes // chunk, states, 0)
@@ -370,7 +396,7 @@
 
     def cell(mean_msg, old, from_state):
         def part(i):
-            return dot(mean_msg, in_v[:, i * width : (i + 1) * width]) + in_b[:, i * width : (i + 1) * width]
+            return dot(mean_msg, in_v[:, i * width : (i + 1) * width]) + in_bias[:, i * width : (i + 1) * width]
 
         reset = jax.nn.sigmoid(part(0) + from_state[:, :width])
         update = jax.nn.sigmoid(part(1) + from_state[:, width : 2 * width])
@@ -433,8 +459,13 @@
         a_next, a_last, b_next, b_last = at(1, 0), at(-1, 0), at(0, 1), at(0, -1)
 
         rows_of[member] = feats
-        for to in (a_next, a_last, b_next, b_last, sibling):
-            send(member, to)
+        for to, which in ((a_next, 0), (a_last, 1), (a_next, 1), (a_last, 0)):
+            send(member, to, which)
+        send(member, b_next, 0)
+        send(member, b_last, 1)
+        send(member, sibling)
+        send(member, b_next, 1)
+        send(member, b_last, 0)
 
         query_w = q_v.at[hop]
         key_w = k_v.at[hop]
@@ -490,62 +521,83 @@
                 parts.append(jnp.concatenate(sides, axis=1))
             acc[...] += dot(jnp.concatenate(parts, axis=0), rows)
 
-        if hop == 0:
-            lax.fori_loop(0, 4, refresh, 0)
-
-        arrive(at(-1, 0))
-        send(at(-1, 0), a_next, 0)
-        for to in (b_next, b_last, sibling):
-            send(at(-1, 0), to)
-        arrive(at(1, 0))
-        send(at(1, 0), a_last, 1)
-        for to in (b_next, b_last, sibling):
-            send(at(1, 0), to)
-        arrive(at(0, -1))
+        lax.fori_loop(hop * 4, hop * 4 + 2, refresh, 0)
+        near, far, across = at(-1, 0), at(1, 0), at(2, 0)
+        arrive(near, 0)
+        send(near, a_next, 0)
+        send(near, b_next, 0)
+        arrive(far, 1)
+        send(far, a_last, 1)
+        send(far, b_last, 1)
+        arrive(near, 1)
+        send(near, b_last, 1)
+        send(near, b_next, 1)
+        arrive(far, 0)
+        send(far, b_next, 0)
+        send(far, b_last, 0)
+        send(near, b_last, 0)
+        send(far, b_next, 1)
+        arrive(at(0, -1), 0)
         send(at(0, -1), b_next, 0)
+        arrive(at(0, 1), 1)
+        send(at(0, 1), b_last, 1)
+        send(near, sibling)
+        send(far, sibling)
+        lax.fori_loop(hop * 4 + 2, hop * 4 + 3, refresh, 0)
+        attend(0, 0)
+        arrive(across, 0)
+        send(across, b_next, 0)
+        arrive(across, 1)
+        send(across, b_last, 1)
+        send(across, b_next, 1)
+        send(across, b_last, 0)
+        send(across, sibling)
+        arrive(at(0, -1), 1)
         send(at(0, -1), sibling)
-        arrive(at(0, 1))
-        send(at(0, 1), b_last, 1)
+        arrive(at(0, 1), 0)
         send(at(0, 1), sibling)
-        attend(0, 0)
-        for which in range(2):
-            arrive(at(2, 0), which)
-        for to in (b_next, b_last, sibling):
-            send(at(2, 0), to)
+        lax.fori_loop(hop * 4 + 3, hop * 4 + 4, refresh, 0)
+        if hop == 1:
+            pass
+        attend(-1, 0)
+        for da in (-1, 1):
+            arrive(at(da, -1), 0)
+            send(at(da, -1), b_next, 0)
+            arrive(at(da, 1), 1)
+            send(at(da, 1), b_last, 1)
+        attend(1, 0)
+        attend(0, -1)
+        for da in (-1, 1):
+            arrive(at(da, -1), 1)
+            send(at(da, -1), sibling)
+            arrive(at(da, 1), 0)
+            send(at(da, 1), sibling)
+        arrive(at(2, -1), 0)
+        send(at(2, -1), b_next, 0)
+        arrive(at(2, 1), 1)
+        send(at(2, 1), b_last, 1)
+        attend(0, 1)
         for which in range(2):
             arrive(at(0, 2), which)
         send(at(0, 2), sibling)
-        if hop == 0:
-            lax.fori_loop(4, 8, refresh, 0)
-        for da, db in ((-1, 0), (1, 0), (0, -1), (0, 1)):
-            attend(da, db)
+        arrive(at(2, -1), 1)
+        send(at(2, -1), sibling)
+        arrive(at(2, 1), 0)
+        send(at(2, 1), sibling)
         for da in (-1, 1):
             for db in (-1, 1):
-                arrive(at(da, db))
-                send(at(da, db), b_next if db == -1 else b_last, 0 if db == -1 else 1)
-                send(at(da, db), sibling)
-        attend(2, 0)
-        attend(0, 2)
-        for db in (-1, 1):
-            arrive(at(2, db))
-            send(at(2, db), b_next if db == -1 else b_last, 0 if db == -1 else 1)
-            send(at(2, db), sibling)
+                attend(da, db)
         for da in (-1, 1):
             for which in range(2):
                 arrive(at(da, 2), which)
             send(at(da, 2), sibling)
-        for da in (-1, 1):
-            for db in (-1, 1):
-                attend(da, db)
+        attend(2, 0)
+        attend(0, 2)
         for which in range(2):
             arrive(at(2, 2), which)
         send(at(2, 2), sibling)
-        for da, db in ((2, -1), (2, 1), (-1, 2), (1, 2)):
+        for da, db in ((2, -1), (2, 1), (-1, 2), (1, 2), (2, 2)):
             attend(da, db)
-        if hop == 0:
-            store = pltpu.make_async_copy(mem, new_memory, out_sem)
-            store.start()
-        attend(2, 2)
 
         value_w = v_v.at[hop]
         mixed = []
@@ -570,7 +622,6 @@
         pltpu.make_async_copy(whole, whole, sends).wait()
 
     embedding[...] = feats
-    store.wait()
 
 
 def on_device(
@@ -608,18 +659,20 @@
     def flat(x):
         return x.reshape(1, -1)
 
+    def rows_of_lanes(x):
+        return x.reshape(-1, LANES)
+
     vmem = pl.BlockSpec(memory_space=pltpu.VMEM)
     hbm = pl.BlockSpec(memory_space=pl.ANY)
     return pl.pallas_call(
         functools.partial(kernel, group_size, device_count),
         out_shape=(
-            jax.ShapeDtypeStruct((nodes, width), F32),
-            jax.ShapeDtypeStruct((queries, width), BF16),
+            pltpu.VMEM((nodes, width), F32),
+            pltpu.VMEM((queries, width), BF16),
         ),
         in_specs=[hbm] + [vmem] * 11 + [hbm, vmem, hbm, hbm, vmem, vmem] + [hbm] * 4 + [vmem],
-        out_specs=(hbm, vmem),
+        out_specs=(vmem, vmem),
         scratch_shapes=[
-            pltpu.VMEM((nodes, width), F32),
             pltpu.VMEM((nodes, width), BF16),
             pltpu.VMEM((nodes, width), BF16),
             pltpu.VMEM(msg_weight.shape, BF16),
@@ -629,8 +682,9 @@
             pltpu.VMEM(key_weight.shape, BF16),
             pltpu.VMEM(value_weight.shape, BF16),
             pltpu.VMEM(merge_weight.shape, BF16),
-            pltpu.VMEM((device_count, 8, LANES), I32),
-            pltpu.VMEM((device_count, 8, LANES), I32),
+            pltpu.VMEM((device_count, 1, LANES), I32),
+            pltpu.VMEM((device_count, 1, LANES), I32),
+            pltpu.VMEM((device_count, LANES), I32),
             pltpu.VMEM((1, slots), F32),
             pltpu.VMEM((device_count, 8, width), BF16),
             pltpu.VMEM((device_count, 8, width), BF16),
@@ -657,7 +711,7 @@
             pltpu.SemaphoreType.DMA((2, group_size, 2)),
         ],
         compiler_params=pltpu.CompilerParams(
-            collective_id=0, has_side_effects=True, vmem_limit_bytes=56 * 2**20
+            collective_id=0, has_side_effects=True, vmem_limit_bytes=54 * 2**20
         ),
     )(
         memory,
@@ -668,16 +722,16 @@
         flat(event_time),
         flat(query_rows),
         flat(link_member),
-        flat(link_slot),
-        flat(link_delta),
+        rows_of_lanes(link_slot),
+        rows_of_lanes(link_delta),
         flat(frequency),
         flat(time_phase),
         msg_weight,
         flat(msg_bias),
         input_weight,
         state_weight,
-        flat(input_bias),
-        flat(state_bias),
+        rows_of_lanes(input_bias),
+        rows_of_lanes(state_bias),
         query_weight,
         key_weight,
         value_weight,

time: 120 us -> 98.7 us (0.82)
  Pallas kernels: 110 us -> 95.9 us
  local copies, waits for them, and re-layouts: 8.95 us -> 1.98 us
    pallas_call x1, Pallas kernels: 110 us -> 95.9 us  [on_device(): pl.pallas_call(functools.partial(kernel, group_size, device_count), out_s...]
    reshape x4 -> x0, local copies, waits for them, and re-layouts: 5.18 us -> none  [flat(): return x.reshape(1, -1)]
    unnamed x4 -> x2, local copies, waits for them, and re-layouts: 3.77 us -> 1.98 us
where the time goes in v2:
time: 98.7 us; the launch traced here: 98.5 us
  Pallas kernels  95.9 us (97%)
  local copies, waits for them, and re-layouts  1.98 us (2%)
    pallas_call x1, Pallas kernels, on_device(): pl.pallas_call(functools.partial(kernel, group_size, device_count), out_s...  95.9 us
    unnamed x2, local copies, waits for them, and re-layouts  1.98 us

profile of v2, /device:TPU:1, one launch (start us, length us, event | category | flops | bytes accessed | tf_op | source)
XLA Modules:
  0.0 98.5 jit_solution(17390162814349310476)
XLA Ops:
  0.6 95.9 %shard_map.230 = (f32[1024,512]{1,0:T(8,128)S(1)}, bf16[128,512]{1,0:T(8,128)(2,1)S(1)}) custom-call(f32[1024,512]{1,0:T(8,128)} %memory.1, s32[1,256]{1,0:T(1,128)} %bitcast.20, s32[1,256]{1,0:T(1,128)} %bitcast.21, s32[1,256]{1,0:T(1,128)} %bitcast.22, s32[1,256]{1,0:T(1,128)} %bitcast.23, s32[1,256]{1,0:T(1,128)} %bitcast.24, s32[1,128]{1,0:T(1,128)} %bitcast.25, ...), custom_call_target="tpu_custom_call" | custom-call | tf_op jit(solution)/shard_map/pallas_call | solution.py:667
  96.5 1.3 %copy.27 = f32[1024,512]{1,0:T(8,128)} copy(f32[1024,512]{1,0:T(8,128)S(1)} %get-tuple-element.2) | data formatting | bytes 4194304
  97.9 0.7 copy.28

commit v3 on v2

--- a/solution.py
+++ b/solution.py
@@ -90,13 +90,13 @@
     m_v,
     req_out,
     req_in,
-    req_rows,
     slot_row,
     xout,
     fetched,
     yout,
     inbound,
     pick,
+    query_pick,
     place,
     msgs,
     back,
@@ -169,17 +169,13 @@
 
     lax.fori_loop(0, device_count - 1, greet, 0)
 
-    places_row, places_col = [], []
+    places_row = []
     for role, owner_ref in enumerate((s_owner, t_owner)):
         own_row = position(owner_ref[...]).astype(F32)
-        own_col = column(own_row)
-        same = own_col == own_row
-        up = iota((events, events), 0) < iota((events, events), 1)
-        down = iota((events, events), 1) < iota((events, events), 0)
-        rank_row = jnp.sum(jnp.where(same & up, 1.0, 0.0), axis=0, keepdims=True)
-        rank_col = jnp.sum(jnp.where(same & down, 1.0, 0.0), axis=1, keepdims=True)
+        earlier = iota((events, events), 0) < iota((events, events), 1)
+        same = column(own_row) == own_row
+        rank_row = jnp.sum(jnp.where(same & earlier, 1.0, 0.0), axis=0, keepdims=True)
         places_row.append(own_row * 8.0 + (rank_row + 4.0 * role))
-        places_col.append(own_col * 8.0 + (rank_col + 4.0 * role))
     place_row = jnp.concatenate(places_row, axis=1).astype(I32)
     wanted_row = jnp.concatenate([s_row[...], t_row[...]], axis=1).astype(F32) + 1.0
 
@@ -210,7 +206,7 @@
                     src_ref=src.at[place],
                     dst_ref=dst.at[place_me],
                     send_sem=send_sem.at[sem],
-                    recv_sem=recv_sem.at[sem],
+                    recv_sem=recv_sem.at[sem, batch],
                     device_id={"group": y, "member": z * 8 + x * 2 + c},
                     device_id_type=MESH,
                 ).start()
@@ -219,9 +215,11 @@
 
         lax.fori_loop(0, 32, one, 0)
 
-    def exchange_wait(src, dst, sem):
-        part = dst.at[pl.ds(0, device_count - 1)]
-        pltpu.make_async_copy(part, part, recv_sem.at[sem]).wait()
+    def arrived(dst, which, own, sem):
+        part = dst.at[pl.ds(0, 31 if own else 32)]
+        pltpu.make_async_copy(part, part, recv_sem.at[sem, which]).wait()
+
+    def sent(src, sem):
         part = src.at[pl.ds(0, device_count - 1)]
         pltpu.make_async_copy(part, part, send_sem.at[sem]).wait()
 
@@ -243,109 +241,6 @@
         return 0
 
     lax.fori_loop(0, nodes // LANES, split, 0)
-
-    exchange_wait(req_out, req_in, 0)
-
-    chunk = 2 * LANES
-    peers = chunk // 8
-    req_rows[...] = req_in[:, 0, :]
-
-    def asked_column(first, count):
-        part = req_rows[pl.ds(first, count), :].astype(F32)
-        spread_out = jnp.broadcast_to(part[:, None, :], (count, 8, LANES))
-        mine_of = iota((count, 8, LANES), 1) == iota((count, 8, LANES), 2)
-        column_of = jnp.sum(jnp.where(mine_of, spread_out, 0.0), axis=2, keepdims=True)
-        return column_of.reshape(count * 8, 1)
-
-    def serve(j, _):
-        c = lax.rem(batch + j + 1, 4)
-        asked = asked_column(pl.multiple_of(c * peers, peers), peers)
-        lane = iota((chunk, LANES), 1).astype(F32)
-        hot = [
-            jnp.where(asked == lane + float(b * LANES), 1.0, 0.0).astype(BF16)
-            for b in range(nodes // LANES)
-        ]
-        rows = dot(jnp.concatenate(hot, axis=1), mem_hi[...])
-        xout[pl.ds(c * peers, peers)] = rows.reshape(peers, 8, width).astype(BF16)
-        exchange(xout, fetched, j + 1, 1)
-        return 0
-
-    lax.fori_loop(0, slots // chunk, serve, 0)
-    fetched[place_me] = xout[place_me]
-
-    lane_slots = iota((events, slots), 1)
-    for role in range(2):
-        hit = lane_slots == places_col[role].astype(I32)
-        pick[pl.ds(role * events, events), :] = jnp.where(hit, 1.0, 0.0).astype(BF16)
-
-    def placing(j, _):
-        hit = place_row == iota((LANES, 2 * events), 0) + j * LANES
-        place[pl.ds(j * LANES, LANES), :] = jnp.where(hit, 1.0, 0.0).astype(BF16)
-        return 0
-
-    lax.fori_loop(0, slots // LANES, placing, 0)
-
-    time_col = column(e_time[...].astype(F32))
-    stamp = cosine(time_col * freq[...] + phase[...]).astype(BF16)
-    for load in loads[1:]:
-        load.wait()
-    stamped = dot(stamp, msg_v[pl.ds(2 * width, LANES), :]) + msg_b[...]
-
-    for b in range(slots // LANES):
-        asked = asked_column(b * 16, 16)
-        diagonal = iota((LANES, LANES), 0) == iota((LANES, LANES), 1)
-        slot_row[:, pl.ds(b * LANES, LANES)] = jnp.sum(
-            jnp.where(diagonal, asked, 0.0), axis=0, keepdims=True
-        )
-
-    def back_matrix(j, _):
-        rows = pl.ds(j * LANES, LANES)
-        node = (iota((LANES, slots), 0) + j * LANES).astype(F32)
-        hot = jnp.where(slot_row[...] == node, 1.0, 0.0)
-        back[rows, :] = hot.astype(BF16)
-        touched[rows, :] = jnp.broadcast_to(
-            jnp.sum(hot, axis=1, keepdims=True), (LANES, LANES)
-        )
-        return 0
-
-    lax.fori_loop(0, nodes // LANES, back_matrix, 0)
-
-    exchange_wait(xout, fetched, 1)
-
-    rows_in = fetched[...].reshape(slots, width)
-    for role in range(2):
-        msgs[pl.ds(role * events, events), :] = dot(
-            pick[pl.ds(role * events, events), :], rows_in
-        ).astype(BF16)
-    source_mem = msgs[pl.ds(0, events), :]
-    target_mem = msgs[pl.ds(events, events), :]
-    first_w = msg_v[pl.ds(0, width), :]
-    second_w = msg_v[pl.ds(width, width), :]
-    to_source = dot(source_mem, first_w) + dot(target_mem, second_w) + stamped
-    to_target = dot(target_mem, first_w) + dot(source_mem, second_w) + stamped
-    msgs[pl.ds(0, events), :] = jnp.maximum(to_source, 0.0).astype(BF16)
-    msgs[pl.ds(events, events), :] = jnp.maximum(to_target, 0.0).astype(BF16)
-
-    def give_back(j, _):
-        c = lax.rem(batch + j + 1, 4)
-        rows = dot(place[pl.ds(c * chunk, chunk), :], msgs[...])
-        yout[pl.ds(c * peers, peers)] = rows.reshape(peers, 8, width).astype(BF16)
-        exchange(yout, inbound, j + 1, 2)
-        return 0
-
-    lax.fori_loop(0, slots // chunk, give_back, 0)
-    inbound[place_me] = yout[place_me]
-
-    query_col = column(q_rows[...].astype(F32))
-    query_hot = jnp.where(
-        iota((queries, nodes), 1).astype(F32) == query_col, 1.0, 0.0
-    ).astype(BF16)
-    query_slots = jnp.where(slot_row[...] == query_col, 1.0, 0.0)
-    query_touched = jnp.sum(query_slots, axis=1, keepdims=True)
-    query_slots = query_slots.astype(BF16)
-    query_hi = dot(query_hot, mem_hi[...])
-    query_mem = query_hi + dot(query_hot, mem_lo[...])
-    query_state = dot(query_hi.astype(BF16), st_v[...]) + st_bias
 
     slot_of = lanes_row(l_slot)
     delta_of = lanes_row(l_delta)
@@ -371,6 +266,70 @@
     member_i = jnp.where(live, member_f, -1.0).astype(I32)
     link_i = member_i * LANES + slot_i
 
+
+    chunk = 2 * LANES
+    peers = chunk // 8
+
+    def asked_column(first, count):
+        part = req_in[pl.ds(first, count), 0, :].astype(F32)
+        spread_out = jnp.broadcast_to(part[:, None, :], (count, 8, LANES))
+        mine_of = iota((count, 8, LANES), 1) == iota((count, 8, LANES), 2)
+        column_of = jnp.sum(jnp.where(mine_of, spread_out, 0.0), axis=2, keepdims=True)
+        return column_of.reshape(count * 8, 1)
+
+    for step in range(1, 5):
+        c = lax.rem(batch + 4 - step, 4)
+        arrived(req_in, c, step == 4, 0)
+        first = pl.multiple_of(c * peers, peers)
+        asked = asked_column(first, peers)
+        lane = iota((chunk, LANES), 1).astype(F32)
+        hot = [
+            jnp.where(asked == lane + float(b * LANES), 1.0, 0.0).astype(BF16)
+            for b in range(nodes // LANES)
+        ]
+        rows = dot(jnp.concatenate(hot, axis=1), mem_hi[...])
+        xout[pl.ds(first, peers)] = rows.reshape(peers, 8, width).astype(BF16)
+        exchange(xout, fetched, 4 - step, 1)
+    fetched[place_me] = xout[place_me]
+
+    for role in range(2):
+        place_col = column(places_row[role])
+        for b in range(4):
+            hit = (iota((events, chunk), 1) + b * chunk).astype(F32) == place_col
+            pick[b, pl.ds(role * events, events), :] = jnp.where(hit, 1.0, 0.0).astype(BF16)
+
+    def placing(j, _):
+        hit = place_row == iota((LANES, 2 * events), 0) + j * LANES
+        place[pl.ds(j * LANES, LANES), :] = jnp.where(hit, 1.0, 0.0).astype(BF16)
+        return 0
+
+    lax.fori_loop(0, slots // LANES, placing, 0)
+
+    time_col = column(e_time[...].astype(F32))
+    stamp = cosine(time_col * freq[...] + phase[...]).astype(BF16)
+    for load in loads[1:]:
+        load.wait()
+    stamped = dot(stamp, msg_v[pl.ds(2 * width, LANES), :]) + msg_b[...]
+
+    for b in range(slots // LANES):
+        asked = asked_column(b * 16, 16)
+        diagonal = iota((LANES, LANES), 0) == iota((LANES, LANES), 1)
+        slot_row[:, pl.ds(b * LANES, LANES)] = jnp.sum(
+            jnp.where(diagonal, asked, 0.0), axis=0, keepdims=True
+        )
+
+    def back_matrix(j, _):
+        rows = pl.ds(j * LANES, LANES)
+        node = (iota((LANES, slots), 0) + j * LANES).astype(F32)
+        hot = jnp.where(slot_row[...] == node, 1.0, 0.0)
+        back[rows, :] = hot.astype(BF16)
+        touched[rows, :] = jnp.broadcast_to(
+            jnp.sum(hot, axis=1, keepdims=True), (LANES, LANES)
+        )
+        return 0
+
+    lax.fori_loop(0, nodes // LANES, back_matrix, 0)
+
     for k in range(FAN):
         code[k] = cosine(delta_f[:, k : k + 1] * freq[...] + phase[...]).astype(BF16)
     self_code = cosine(phase[...]).astype(BF16)
@@ -385,6 +344,42 @@
 
     lax.fori_loop(0, group_size, invert, 0)
 
+    sent(req_out, 0)
+
+    pairs = jnp.zeros((2 * events, width), F32)
+    for step in range(1, 5):
+        c = lax.rem(batch + step, 4)
+        arrived(fetched, c, step == 4, 1)
+        rows = fetched[pl.ds(pl.multiple_of(c * peers, peers), peers)].reshape(chunk, width)
+        pairs = pairs + dot(pick[c], rows)
+    pairs = pairs.astype(BF16)
+    swapped = jnp.concatenate([pairs[events:], pairs[:events]], axis=0)
+    out = dot(pairs, msg_v[pl.ds(0, width), :]) + dot(swapped, msg_v[pl.ds(width, width), :])
+    msgs[...] = jnp.maximum(out + jnp.concatenate([stamped, stamped], axis=0), 0.0).astype(BF16)
+
+    def give_back(j, _):
+        c = lax.rem(batch + j + 1, 4)
+        rows = dot(place[pl.ds(c * chunk, chunk), :], msgs[...])
+        yout[pl.ds(c * peers, peers)] = rows.reshape(peers, 8, width).astype(BF16)
+        exchange(yout, inbound, j + 1, 2)
+        return 0
+
+    lax.fori_loop(0, slots // chunk, give_back, 0)
+    inbound[place_me] = yout[place_me]
+
+    query_col = column(q_rows[...].astype(F32))
+    query_hot = jnp.where(
+        iota((queries, nodes), 1).astype(F32) == query_col, 1.0, 0.0
+    ).astype(BF16)
+    query_touched = jnp.zeros((queries, 1), F32)
+    for b in range(4):
+        hit = jnp.where(slot_row[:, b * chunk : (b + 1) * chunk] == query_col, 1.0, 0.0)
+        query_touched = query_touched + jnp.sum(hit, axis=1, keepdims=True)
+        query_pick[b] = hit.astype(BF16)
+    query_hi = dot(query_hot, mem_hi[...])
+    query_mem = query_hi + dot(query_hot, mem_lo[...])
+    query_state = dot(query_hi.astype(BF16), st_v[...]) + st_bias
+
     def states(j, _):
         rows = pl.ds(j * chunk, chunk)
         state[rows, :] = dot(mem_hi[rows, :], st_v[...]) + st_bias
@@ -392,7 +387,7 @@
 
     lax.fori_loop(0, nodes // chunk, states, 0)
 
-    exchange_wait(yout, inbound, 2)
+    sent(xout, 1)
 
     def cell(mean_msg, old, from_state):
         def part(i):
@@ -403,8 +398,13 @@
         candidate = jnp.tanh(part(2) + reset * from_state[:, 2 * width :])
         return (1.0 - update) * candidate + update * old
 
-    messages_in = inbound[...].reshape(slots, width)
-    query_mean = (dot(query_slots, messages_in) / jnp.maximum(query_touched, 1.0)).astype(BF16)
+    query_sum = jnp.zeros((queries, width), F32)
+    for step in range(1, 5):
+        c = lax.rem(batch + 4 - step, 4)
+        arrived(inbound, c, step == 4, 2)
+        rows = inbound[pl.ds(pl.multiple_of(c * peers, peers), peers)].reshape(chunk, width)
+        query_sum = query_sum + dot(query_pick[c], rows)
+    query_mean = (query_sum / jnp.maximum(query_touched, 1.0)).astype(BF16)
     fresh = cell(query_mean, query_mem, query_state)
     feats = jnp.where(query_touched > 0.0, fresh, query_mem).astype(BF16)
 
@@ -622,6 +622,7 @@
         pltpu.make_async_copy(whole, whole, sends).wait()
 
     embedding[...] = feats
+    sent(yout, 2)
 
 
 def on_device(
@@ -684,13 +685,13 @@
             pltpu.VMEM(merge_weight.shape, BF16),
             pltpu.VMEM((device_count, 1, LANES), I32),
             pltpu.VMEM((device_count, 1, LANES), I32),
-            pltpu.VMEM((device_count, LANES), I32),
             pltpu.VMEM((1, slots), F32),
             pltpu.VMEM((device_count, 8, width), BF16),
             pltpu.VMEM((device_count, 8, width), BF16),
             pltpu.VMEM((device_count, 8, width), BF16),
             pltpu.VMEM((device_count, 8, width), BF16),
-            pltpu.VMEM((2 * events, slots), BF16),
+            pltpu.VMEM((4, 2 * events, slots // 4), BF16),
+            pltpu.VMEM((4, queries, slots // 4), BF16),
             pltpu.VMEM((slots, 2 * events), BF16),
             pltpu.VMEM((2 * events, width), BF16),
             pltpu.VMEM((nodes, slots), BF16),
@@ -706,7 +707,7 @@
             pltpu.SemaphoreType.DMA((8,)),
             pltpu.SemaphoreType.DMA,
             pltpu.SemaphoreType.DMA((3,)),
-            pltpu.SemaphoreType.DMA((3,)),
+            pltpu.SemaphoreType.DMA((3, 4)),
             pltpu.SemaphoreType.DMA((2,)),
             pltpu.SemaphoreType.DMA((2, group_size, 2)),
         ],

time: 98.7 us -> 94.8 us (0.960)
  Pallas kernels: 95.9 us -> 92 us
    pallas_call x1, Pallas kernels: 95.9 us -> 92 us  [on_device(): pl.pallas_call(functools.partial(kernel, group_size, device_count), out_s...]
where the time goes in v3:
time: 94.8 us; the launch traced here: 94.6 us
  Pallas kernels  92 us (97%)
  local copies, waits for them, and re-layouts  1.98 us (2%)
    pallas_call x1, Pallas kernels, on_device(): pl.pallas_call(functools.partial(kernel, group_size, device_count), out_s...  92 us
    unnamed x2, local copies, waits for them, and re-layouts  1.98 us

profile of v3, /device:TPU:1, one launch (start us, length us, event | category | flops | bytes accessed | tf_op | source)
XLA Modules:
  0.0 94.6 jit_solution(14753856070858310146)
XLA Ops:
  0.6 92.0 %shard_map.230 = (f32[1024,512]{1,0:T(8,128)S(1)}, bf16[128,512]{1,0:T(8,128)(2,1)S(1)}) custom-call(f32[1024,512]{1,0:T(8,128)} %memory.1, s32[1,256]{1,0:T(1,128)} %bitcast.20, s32[1,256]{1,0:T(1,128)} %bitcast.21, s32[1,256]{1,0:T(1,128)} %bitcast.22, s32[1,256]{1,0:T(1,128)} %bitcast.23, s32[1,256]{1,0:T(1,128)} %bitcast.24, s32[1,128]{1,0:T(1,128)} %bitcast.25, ...), custom_call_target="tpu_custom_call" | custom-call | tf_op jit(solution)/shard_map/pallas_call | solution.py:668
  92.6 1.3 %copy.27 = f32[1024,512]{1,0:T(8,128)} copy(f32[1024,512]{1,0:T(8,128)S(1)} %get-tuple-element.2) | data formatting | bytes 4194304
  94.0 0.7 copy.28

commit v4 on v3

--- a/solution.py
+++ b/solution.py
@@ -191,29 +191,41 @@
     pl.semaphore_wait(barrier, device_count - 1)
 
     def exchange(src, dst, j, sem):
-        def one(i, _):
-            q = lax.rem(lax.rem(i, 16) * 7, 16)
+        def hops(q):
+            steps = (q // 4, q % 4, (j - q // 4 - q % 4) % 4)
+            return sum(min(s, 4 - s) for s in steps)
+
+        order = sorted(range(16), key=lambda q: (-hops(q), q * 7 % 16))
+        k = lax.rem(batch + j, 4)
+
+        def one(i, rest):
+            q = lax.rem(rest, 16)
             y = lax.rem(group + lax.div(q, 4), 4)
             z = lax.rem(z_pos + lax.rem(q, 4), 4)
-            c = lax.rem(core + i + lax.div(i, 16), 2)
-            k = lax.rem(batch + j, 4)
             x = lax.rem(k - y - z + 8, 4)
-            place = k * 32 + y * 8 + z * 2 + c
-
-            @pl.when(place != place_me)
-            def _():
-                pltpu.make_async_remote_copy(
-                    src_ref=src.at[place],
-                    dst_ref=dst.at[place_me],
-                    send_sem=send_sem.at[sem],
-                    recv_sem=recv_sem.at[sem, batch],
-                    device_id={"group": y, "member": z * 8 + x * 2 + c},
-                    device_id_type=MESH,
-                ).start()
-
-            return 0
-
-        lax.fori_loop(0, 32, one, 0)
+            for flip in range(2):
+                c = lax.rem(core + i + flip, 2)
+                place = k * 32 + y * 8 + z * 2 + c
+
+                def go():
+                    pltpu.make_async_remote_copy(
+                        src_ref=src.at[place],
+                        dst_ref=dst.at[place_me],
+                        send_sem=send_sem.at[sem],
+                        recv_sem=recv_sem.at[sem, batch],
+                        device_id={"group": y, "member": z * 8 + x * 2 + c},
+                        device_id_type=MESH,
+                    ).start()
+
+                if j % 4 == 0:
+                    pl.when(place != place_me)(go)
+                else:
+                    go()
+            return lax.div(rest, 16)
+
+        for first in range(0, 16, 4):
+            packed = sum(q * 16**i for i, q in enumerate(order[first : first + 4]))
+            lax.fori_loop(0, 4, one, jnp.int32(packed))
 
     def arrived(dst, which, own, sem):
         part = dst.at[pl.ds(0, 31 if own else 32)]
@@ -223,11 +235,8 @@
         part = src.at[pl.ds(0, device_count - 1)]
         pltpu.make_async_copy(part, part, send_sem.at[sem]).wait()
 
-    def send_requests(j, _):
-        exchange(req_out, req_in, j + 1, 0)
-        return 0
-
-    lax.fori_loop(0, 4, send_requests, 0)
+    for step in range(1, 5):
+        exchange(req_out, req_in, step, 0)
     req_in[place_me] = req_out[place_me]
 
     loads[0].wait()
@@ -237,7 +246,11 @@
         x = mem[rows, :]
         hi = x.astype(BF16)
         mem_hi[rows, :] = hi
-        mem_lo[rows, :] = (x - hi.astype(F32)).astype(BF16)
+        return 0
+
+    def remainder(j, _):
+        rows = pl.ds(j * LANES, LANES)
+        mem_lo[rows, :] = (mem[rows, :] - mem_hi[rows, :].astype(F32)).astype(BF16)
         return 0
 
     lax.fori_loop(0, nodes // LANES, split, 0)
@@ -357,16 +370,15 @@
     out = dot(pairs, msg_v[pl.ds(0, width), :]) + dot(swapped, msg_v[pl.ds(width, width), :])
     msgs[...] = jnp.maximum(out + jnp.concatenate([stamped, stamped], axis=0), 0.0).astype(BF16)
 
-    def give_back(j, _):
-        c = lax.rem(batch + j + 1, 4)
-        rows = dot(place[pl.ds(c * chunk, chunk), :], msgs[...])
+    for step in range(1, 5):
+        c = lax.rem(batch + step, 4)
+        rows = dot(place[pl.ds(pl.multiple_of(c * chunk, chunk), chunk), :], msgs[...])
         yout[pl.ds(c * peers, peers)] = rows.reshape(peers, 8, width).astype(BF16)
-        exchange(yout, inbound, j + 1, 2)
-        return 0
-
-    lax.fori_loop(0, slots // chunk, give_back, 0)
+        exchange(yout, inbound, step, 2)
+
     inbound[place_me] = yout[place_me]
 
+    lax.fori_loop(0, nodes // LANES, remainder, 0)
     query_col = column(q_rows[...].astype(F32))
     query_hot = jnp.where(
         iota((queries, nodes), 1).astype(F32) == query_col, 1.0, 0.0

time: 94.8 us -> 92.9 us (0.980)
  Pallas kernels: 92 us -> 90.1 us
    pallas_call x1, Pallas kernels: 92 us -> 90.1 us  [on_device(): pl.pallas_call(functools.partial(kernel, group_size, device_count), out_s...]
where the time goes in v4:
time: 92.9 us; the launch traced here: 92.7 us
  Pallas kernels  90.1 us (97%)
  local copies, waits for them, and re-layouts  1.98 us (2%)
    pallas_call x1, Pallas kernels, on_device(): pl.pallas_call(functools.partial(kernel, group_size, device_count), out_s...  90.1 us
    unnamed x2, local copies, waits for them, and re-layouts  1.98 us

profile of v4, /device:TPU:1, one launch (start us, length us, event | category | flops | bytes accessed | tf_op | source)
XLA Modules:
  0.0 92.7 jit_solution(3976824123781767549)
XLA Ops:
  0.6 90.1 %shard_map.230 = (f32[1024,512]{1,0:T(8,128)S(1)}, bf16[128,512]{1,0:T(8,128)(2,1)S(1)}) custom-call(f32[1024,512]{1,0:T(8,128)} %memory.1, s32[1,256]{1,0:T(1,128)} %bitcast.20, s32[1,256]{1,0:T(1,128)} %bitcast.21, s32[1,256]{1,0:T(1,128)} %bitcast.22, s32[1,256]{1,0:T(1,128)} %bitcast.23, s32[1,256]{1,0:T(1,128)} %bitcast.24, s32[1,128]{1,0:T(1,128)} %bitcast.25, ...), custom_call_target="tpu_custom_call" | custom-call | tf_op jit(solution)/shard_map/pallas_call | solution.py:680
  90.8 1.3 %copy.27 = f32[1024,512]{1,0:T(8,128)} copy(f32[1024,512]{1,0:T(8,128)S(1)} %get-tuple-element.2) | data formatting | bytes 4194304
  92.1 0.7 copy.28
